TPU v7x, 32 devices: a whole 2x2x4 slice. The times are simulated.
32 devices in a mesh: dp: 8 (over z, y), mp: 4 (over x, core).
Axes of the slice: x: 2, y: 2, z: 4, core: 2. Of those that a mesh axis runs over, the one named last changes fastest.
Arguments:
- tokens: bfloat16 [16384, 768], P(('dp', 'mp')), may hold values from -6 to 6
- w_query: bfloat16 [768, 768], P('dp', 'mp'), may hold values from -0.109375 to 0.109375
- w_key: bfloat16 [768, 768], P('dp', 'mp'), may hold values from -0.109375 to 0.109375
- w_value: bfloat16 [768, 768], P('dp', 'mp'), may hold values from -0.21875 to 0.21875
- w_out: bfloat16 [768, 768], P('dp', 'mp'), may hold values from -0.625 to 0.625
- w_gate: bfloat16 [768, 2048], P('dp', 'mp'), may hold values from -0.21875 to 0.21875
- w_up: bfloat16 [768, 2048], P('dp', 'mp'), may hold values from -0.21875 to 0.21875
- w_down: bfloat16 [768, 2048], P('dp', 'mp'), may hold values from -0.125 to 0.125
- norm_attn: float32 [768], replicated, may hold values from 0.5 to 1.5
- norm_mlp: float32 [768], replicated, may hold values from 0.5 to 1.5
- valid_counts: int32 [8], P('dp'), may hold values from 512 to 2048
- group_ids: int32 [8, 2048], P('dp'), may hold values from 0 to 3, never falling along the last dimension, each value on 1 to 1024 neighbouring positions
- cotangent: bfloat16 [16384, 768], P(('dp', 'mp')), may hold values from -6 to 6
Outputs:
- output: bfloat16 [16384, 768], P(('dp', 'mp'))
- grad_tokens: bfloat16 [16384, 768], P(('dp', 'mp'))
- grad_query: float32 [768, 768], P('dp', 'mp')
- grad_key: float32 [768, 768], P('dp', 'mp')
- grad_value: float32 [768, 768], P('dp', 'mp')
- grad_out: float32 [768, 768], P('dp', 'mp')
- grad_gate: float32 [768, 2048], P('dp', 'mp')
- grad_up: float32 [768, 2048], P('dp', 'mp')
- grad_down: float32 [768, 2048], P('dp', 'mp')
- grad_norm_attn: float32 [768], replicated
- grad_norm_mlp: float32 [768], replicated
Inputs may be any that keep to these rules, and one draw needn't show every extreme that they name: `group_ids`: in each image the ids never fall, start at 0 and reach 3; each group has 1 to 1024 patches.
All inputs are finite; a program needn't handle non-finite values.
Results may differ from a plain program's by a relative error of at most 0.02.
Values may be sent and summed in bfloat16 or wider, within the bound.
No kernel may reach another device: no remote copies, remote signals or barrier semaphores. Data moves between devices by JAX's collectives and lax.ppermute only.
A program may use at most 128 MiB of HBM per device.

v0:
```python
import jax
import jax.numpy as jnp
from jax import lax
from jax.sharding import PartitionSpec as P

HEAD = 64
BLOCK = 512


eps_norm = 1e-06
neg_large = -1e30


def rms_scale(values):
    return lax.rsqrt(jnp.mean(values * values, axis=-1, keepdims=True) + eps_norm)


def rms_back(values, scale, gain, grad_normed):
    grad_hat = grad_normed * gain
    return scale * grad_hat - values * (scale * scale * scale) * jnp.mean(
        grad_hat * values, axis=-1, keepdims=True
    )


def product(matrix_one, matrix_two):
    return jnp.dot(matrix_one, matrix_two, preferred_element_type=jnp.float32)


def product_trans(matrix_one, matrix_two):
    return lax.dot_general(
        matrix_one, matrix_two, (((1,), (1,)), ((), ())), preferred_element_type=jnp.float32
    )


def rows_product(matrix_one, matrix_two):
    return lax.dot_general(
        matrix_one, matrix_two, (((0,), (0,)), ((), ())), preferred_element_type=jnp.float32
    )


def masked_scores(query_blk, key_heads, first_row, groups, valid_count):
    scores = jnp.einsum("qhd,khd->hqk", query_blk, key_heads, preferred_element_type=jnp.float32)
    row_count = query_blk.shape[0]
    key_index = jnp.arange(key_heads.shape[0], dtype=jnp.int32)
    row_index = first_row + jnp.arange(row_count, dtype=jnp.int32)
    row_groups = lax.dynamic_slice_in_dim(groups, first_row, row_count)
    same_group = row_groups[:, None] == groups[None, :]
    usable = (key_index < valid_count)[None, :] | (row_index[:, None] == key_index[None, :])
    return jnp.where((same_group & usable)[None], scores, neg_large)


def image_forward(queries, keys_all, values_all, groups, valid_count):
    length = queries.shape[0]
    head_count = queries.shape[1] // HEAD
    key_heads = keys_all.reshape(length, head_count, HEAD)
    value_heads = values_all.reshape(length, head_count, HEAD)
    blocks = length // BLOCK
    query_blocks = queries.reshape(blocks, BLOCK, head_count, HEAD)

    def one_block(carry, block_items):
        query_blk, block_index = block_items
        scores = masked_scores(query_blk, key_heads, block_index * BLOCK, groups, valid_count)
        top_score = jnp.max(scores, axis=-1, keepdims=True)
        expanded = jnp.exp(scores - top_score)
        summed = jnp.sum(expanded, axis=-1, keepdims=True)
        weights_p = (expanded / summed).astype(jnp.bfloat16)
        result = jnp.einsum(
            "hqk,khd->qhd", weights_p, value_heads, preferred_element_type=jnp.float32
        )
        return (
            carry,
            (result.reshape(BLOCK, head_count * HEAD), (top_score + jnp.log(summed))[..., 0]),
        )

    carry, (results, log_sums) = lax.scan(
        one_block, None, (query_blocks, jnp.arange(blocks, dtype=jnp.int32))
    )
    return (results.reshape(length, head_count * HEAD), log_sums)


def image_backward(queries, keys_all, values_all, grad_att, log_sums, groups, valid_count):
    length = queries.shape[0]
    head_count = queries.shape[1] // HEAD
    key_heads = keys_all.reshape(length, head_count, HEAD)
    value_heads = values_all.reshape(length, head_count, HEAD)
    blocks = length // BLOCK
    query_blocks = queries.reshape(blocks, BLOCK, head_count, HEAD)
    grad_blocks = grad_att.reshape(blocks, BLOCK, head_count, HEAD)
    zeros_kv = jnp.zeros((length, head_count, HEAD), jnp.float32)

    def one_block(carry, block_items):
        grad_keys, grad_values = carry
        query_blk, grad_blk, log_blk, block_index = block_items
        scores = masked_scores(query_blk, key_heads, block_index * BLOCK, groups, valid_count)
        weights_p = jnp.exp(scores - log_blk[..., None])
        grad_p = jnp.einsum(
            "qhd,khd->hqk", grad_blk, value_heads, preferred_element_type=jnp.float32
        )
        delta_row = jnp.sum(weights_p * grad_p, axis=-1, keepdims=True)
        grad_scores = (weights_p * (grad_p - delta_row)).astype(jnp.bfloat16)
        grad_rows = jnp.einsum(
            "hqk,khd->qhd", grad_scores, key_heads, preferred_element_type=jnp.float32
        )
        grad_keys = grad_keys + jnp.einsum(
            "hqk,qhd->khd", grad_scores, query_blk, preferred_element_type=jnp.float32
        )
        grad_values = grad_values + jnp.einsum(
            "hqk,qhd->khd",
            weights_p.astype(jnp.bfloat16),
            grad_blk,
            preferred_element_type=jnp.float32,
        )
        return ((grad_keys, grad_values), grad_rows.reshape(BLOCK, head_count * HEAD))

    (grad_keys, grad_values), grad_rows = lax.scan(
        one_block,
        (zeros_kv, zeros_kv),
        (query_blocks, grad_blocks, log_sums, jnp.arange(blocks, dtype=jnp.int32)),
    )
    width = head_count * HEAD
    return (
        grad_rows.reshape(length, width).astype(jnp.bfloat16),
        grad_keys.reshape(length, width).astype(jnp.bfloat16),
        grad_values.reshape(length, width).astype(jnp.bfloat16),
    )


def local(
    tokens,
    w_query,
    w_key,
    w_value,
    w_out,
    w_gate,
    w_up,
    w_down,
    norm_attn,
    norm_mlp,
    valid_counts,
    group_ids,
    cotangent,
):
    gathered = (
        lax.all_gather(w_query, "dp", axis=0, tiled=True),
        lax.all_gather(w_key, "dp", axis=0, tiled=True),
        lax.all_gather(w_value, "dp", axis=0, tiled=True),
        lax.all_gather(w_out, "dp", axis=0, tiled=True),
        lax.all_gather(w_gate, "dp", axis=0, tiled=True),
        lax.all_gather(w_up, "dp", axis=0, tiled=True),
        lax.all_gather(w_down, "dp", axis=0, tiled=True),
    )
    full_q, full_k, full_v, full_o, full_g, full_u, full_d = gathered
    images = valid_counts.shape[0]
    head_cols = full_q.shape[1]
    inputs = tokens.astype(jnp.float32)
    scale_attn = rms_scale(inputs)
    normed_rows = (inputs * scale_attn * norm_attn).astype(jnp.bfloat16)
    normed_attn = lax.all_gather(normed_rows, "mp", axis=0, tiled=True)
    queries = product(normed_attn, full_q).astype(jnp.bfloat16)
    keys_all = product(normed_attn, full_k).astype(jnp.bfloat16)
    values_all = product(normed_attn, full_v).astype(jnp.bfloat16)
    attended, log_sums = lax.map(
        lambda image_items: image_forward(*image_items),
        (
            queries.reshape(images, -1, head_cols),
            keys_all.reshape(images, -1, head_cols),
            values_all.reshape(images, -1, head_cols),
            group_ids,
            valid_counts,
        ),
    )
    attended = attended.reshape(-1, head_cols).astype(jnp.bfloat16)
    attn_rows = lax.psum_scatter(
        product_trans(attended, full_o).astype(jnp.bfloat16), "mp", scatter_dimension=0, tiled=True
    ).astype(jnp.float32)
    middle = inputs + attn_rows
    scale_mlp = rms_scale(middle)
    normed_rows_two = (middle * scale_mlp * norm_mlp).astype(jnp.bfloat16)
    normed_mlp = lax.all_gather(normed_rows_two, "mp", axis=0, tiled=True)
    gate_pre = product(normed_mlp, full_g)
    up_pre = product(normed_mlp, full_u)
    hidden = (jax.nn.gelu(gate_pre, approximate=True) * up_pre).astype(jnp.bfloat16)
    mlp_rows = lax.psum_scatter(
        product_trans(hidden, full_d).astype(jnp.bfloat16), "mp", scatter_dimension=0, tiled=True
    ).astype(jnp.float32)
    output = (middle + mlp_rows).astype(jnp.bfloat16)
    grad_mixed = lax.all_gather(cotangent, "mp", axis=0, tiled=True)
    grad_down = rows_product(grad_mixed, hidden)
    grad_hidden = product(grad_mixed, full_d)
    gelu_value, gelu_pull = jax.vjp(
        lambda gate_in: jax.nn.gelu(gate_in, approximate=True), gate_pre
    )
    grad_gate_pre = gelu_pull(grad_hidden * up_pre)[0].astype(jnp.bfloat16)
    grad_up_pre = (grad_hidden * gelu_value).astype(jnp.bfloat16)
    grad_gate = rows_product(normed_mlp, grad_gate_pre)
    grad_up = rows_product(normed_mlp, grad_up_pre)
    grad_normed_mlp = lax.psum_scatter(
        (product_trans(grad_gate_pre, full_g) + product_trans(grad_up_pre, full_u)).astype(
            jnp.bfloat16
        ),
        "mp",
        scatter_dimension=0,
        tiled=True,
    ).astype(jnp.float32)
    grad_middle = cotangent.astype(jnp.float32) + rms_back(
        middle, scale_mlp, norm_mlp, grad_normed_mlp
    )
    gain_mlp_part = jnp.sum(grad_normed_mlp * middle * scale_mlp, axis=0)
    grad_attn = lax.all_gather(grad_middle.astype(jnp.bfloat16), "mp", axis=0, tiled=True)
    grad_out = rows_product(grad_attn, attended)
    grad_attended = product(grad_attn, full_o).astype(jnp.bfloat16)
    grad_q, grad_k, grad_v = lax.map(
        lambda image_items: image_backward(*image_items),
        (
            queries.reshape(images, -1, head_cols),
            keys_all.reshape(images, -1, head_cols),
            values_all.reshape(images, -1, head_cols),
            grad_attended.reshape(images, -1, head_cols),
            log_sums,
            group_ids,
            valid_counts,
        ),
    )
    grad_q = grad_q.reshape(-1, head_cols)
    grad_k = grad_k.reshape(-1, head_cols)
    grad_v = grad_v.reshape(-1, head_cols)
    grad_query = rows_product(normed_attn, grad_q)
    grad_key = rows_product(normed_attn, grad_k)
    grad_value = rows_product(normed_attn, grad_v)
    grad_normed_attn = lax.psum_scatter(
        (
            product_trans(grad_q, full_q)
            + product_trans(grad_k, full_k)
            + product_trans(grad_v, full_v)
        ).astype(jnp.bfloat16),
        "mp",
        scatter_dimension=0,
        tiled=True,
    ).astype(jnp.float32)
    grad_tokens = (grad_middle + rms_back(inputs, scale_attn, norm_attn, grad_normed_attn)).astype(
        jnp.bfloat16
    )
    gain_attn_part = jnp.sum(grad_normed_attn * inputs * scale_attn, axis=0)
    gain_attn, gain_mlp = lax.psum((gain_attn_part, gain_mlp_part), ("dp", "mp"))
    shares = (
        lax.psum_scatter(grad_query, "dp", scatter_dimension=0, tiled=True),
        lax.psum_scatter(grad_key, "dp", scatter_dimension=0, tiled=True),
        lax.psum_scatter(grad_value, "dp", scatter_dimension=0, tiled=True),
        lax.psum_scatter(grad_out, "dp", scatter_dimension=0, tiled=True),
        lax.psum_scatter(grad_gate, "dp", scatter_dimension=0, tiled=True),
        lax.psum_scatter(grad_up, "dp", scatter_dimension=0, tiled=True),
        lax.psum_scatter(grad_down, "dp", scatter_dimension=0, tiled=True),
    )
    return (
        output,
        grad_tokens,
        shares[0],
        shares[1],
        shares[2],
        shares[3],
        shares[4],
        shares[5],
        shares[6],
        gain_attn,
        gain_mlp,
    )


def solution(mesh):
    return jax.shard_map(
        local,
        mesh=mesh,
        in_specs=(
            P(("dp", "mp"), None),
            P("dp", "mp"),
            P("dp", "mp"),
            P("dp", "mp"),
            P("dp", "mp"),
            P("dp", "mp"),
            P("dp", "mp"),
            P("dp", "mp"),
            P(),
            P(),
            P("dp"),
            P("dp", None),
            P(("dp", "mp"), None),
        ),
        out_specs=(
            P(("dp", "mp"), None),
            P(("dp", "mp"), None),
            P("dp", "mp"),
            P("dp", "mp"),
            P("dp", "mp"),
            P("dp", "mp"),
            P("dp", "mp"),
            P("dp", "mp"),
            P("dp", "mp"),
            P(),
            P(),
        ),
        check_vma=False,
    )
```

profile of v0, /device:TPU:0, one launch (start us, length us, event | category | flops | bytes accessed | tf_op | source)
XLA Modules:
  0.0 1194.4 jit_solution(7332878798178661854)
XLA Ops:
  11.6 33.1 %all_gather.34 = bf16[768,192]{1,0:T(8,128)(2,1)S(1)} all-gather(bf16[96,192]{1,0:T(8,128)(2,1)S(1)} %copy-done.40), channel_id=1, replica_groups=mesh['dp'=8,'mp'=4] {'dp'}, dimensions={0}, use_global_device_ids=true | all-gather | bytes 331776 | tf_op jit(solution)/shard_map/all_gather | solution.py:144
  44.7 31.0 %all_gather.35 = bf16[768,192]{1,0:T(8,128)(2,1)S(1)} all-gather(bf16[96,192]{1,0:T(8,128)(2,1)S(1)} %copy-done.41), channel_id=1, replica_groups=mesh['dp'=8,'mp'=4] {'dp'}, dimensions={0}, use_global_device_ids=true | all-gather | bytes 331776 | tf_op jit(solution)/shard_map/all_gather | solution.py:145
  75.6 31.1 %all_gather.36 = bf16[768,192]{1,0:T(8,128)(2,1)S(1)} all-gather(bf16[96,192]{1,0:T(8,128)(2,1)S(1)} %copy-done.42), channel_id=1, replica_groups=mesh['dp'=8,'mp'=4] {'dp'}, dimensions={0}, use_global_device_ids=true | all-gather | bytes 331776 | tf_op jit(solution)/shard_map/all_gather | solution.py:146
  106.7 31.0 %all_gather.37 = bf16[768,192]{1,0:T(8,128)(2,1)S(1)} all-gather(bf16[96,192]{1,0:T(8,128)(2,1)S(1)} %copy-done.43), channel_id=1, replica_groups=mesh['dp'=8,'mp'=4] {'dp'}, dimensions={0}, use_global_device_ids=true | all-gather | bytes 331776 | tf_op jit(solution)/shard_map/all_gather | solution.py:147
  146.9 103.1 %while.47 = (s32[]{:T(128)}, bf16[4,512,192]{1,2,0:T(8,128)(2,1)}, f32[4,3,512]{2,1,0:T(4,128)}, s32[4]{0:T(128)S(1)}, s32[2048]{0:T(1024)S(1)}, /*index=5*/s32[...) while((s32[]{:T(128)}, bf16[4,512,192]{1,2,0:T(8,128)(2,1)}, ...), condition=%wide.region_4.5_spmd, body=%wide.region_1.4_spmd.sunk | while | flops 837813248 | bytes 44376280 | solution.py:75
  150.9 6.7 select_reduce_fusion.2
  157.6 7.8 fusion.148
  176.6 6.7 select_reduce_fusion.2
  183.3 7.8 fusion.148
  191.0 6.4 fusion.149
  202.2 6.7 select_reduce_fusion.2
  208.9 7.8 fusion.148
  216.6 6.4 fusion.149
  227.8 6.7 select_reduce_fusion.2
  234.5 7.8 fusion.148
  242.3 6.4 fusion.149
  254.3 39.1 %reduce-scatter.14.cloned.1.call-done = bf16[512,768]{1,0:T(8,128)(2,1)} async-done(((bf16[2048,768]{1,0:T(8,128)(2,1)}), bf16[512,768]{1,0:T(8,128)(2,1)}) %reduce-scatter.14.cloned.1.call-update) | async-done | bytes 786448 | tf_op jit(solution)/shard_map/reduce_scatter | solution.py:173
  298.5 34.2 %all_gather.39 = bf16[768,512]{1,0:T(8,128)(2,1)} all-gather(bf16[96,512]{1,0:T(8,128)(2,1)S(1)} %copy-done.35), channel_id=1, replica_groups=mesh['dp'=8,'mp'=4] {'dp'}, dimensions={0}, use_global_device_ids=true | all-gather | bytes 884736 | tf_op jit(solution)/shard_map/all_gather | solution.py:148
  332.7 32.5 %all_gather.40 = bf16[768,512]{1,0:T(8,128)(2,1)S(1)} all-gather(bf16[96,512]{1,0:T(8,128)(2,1)} %param.23), channel_id=1, replica_groups=mesh['dp'=8,'mp'=4] {'dp'}, dimensions={0}, use_global_device_ids=true | all-gather | bytes 884736 | tf_op jit(solution)/shard_map/all_gather | solution.py:149
  365.2 34.3 %all_gather.41 = bf16[768,512]{1,0:T(8,128)(2,1)} all-gather(bf16[96,512]{1,0:T(8,128)(2,1)} %param.24), channel_id=1, replica_groups=mesh['dp'=8,'mp'=4] {'dp'}, dimensions={0}, use_global_device_ids=true | all-gather | bytes 884736 | tf_op jit(solution)/shard_map/all_gather | solution.py:150
  409.3 9.3 multiply_convert_fusion.1
  424.3 38.1 %reduce-scatter.18.cloned.1.call-done = bf16[512,768]{1,0:T(8,128)(2,1)} async-done(((bf16[2048,768]{1,0:T(8,128)(2,1)}), bf16[512,768]{1,0:T(8,128)(2,1)}) %reduce-scatter.18.cloned.1.call-update) | async-done | bytes 786448 | tf_op jit(solution)/shard_map/reduce_scatter | solution.py:197
  468.3 28.6 %all-gather.11.cloned.1.call-done = bf16[2048,768]{1,0:T(8,128)(2,1)} async-done(((bf16[512,768]{1,0:T(8,128)(2,1)}), bf16[2048,768]{1,0:T(8,128)(2,1)}) %all-gather.11.cloned.1.call-update) | async-done | bytes 3145744 | tf_op jit(solution)/shard_map/all_gather | solution.py:209
  501.7 130.5 %while.48 = (s32[]{:T(128)}, f32[2048,3,64]{0,2,1:T(8,128)}, f32[2048,3,64]{0,2,1:T(8,128)}, bf16[4,512,192]{1,2,0:T(8,128)(2,1)}, bf16[4,512,3,64]{1,3,2,0:T(8,...) while((s32[]{:T(128)}, f32[2048,3,64]{0,2,1:T(8,128)}, ...), condition=%wide.region_12.13_spmd.clone, body=%wide.region_10.12_spmd.clone.sunk | while | flops 2056782848 | bytes 156895728 | solution.py:115
  684.0 39.8 %all-reduce = (f32[768]{0:T(1024)}, f32[768]{0:T(1024)}) all-reduce(f32[768]{0:T(1024)S(1)} %get-tuple-element.322, f32[768]{0:T(1024)S(1)} %copy-done.50), channel_id=1, replica_groups=mesh['dp'=8,'mp'=4] {'dp','mp'}, use_global_device_ids=true, to_apply=%region_23.24 | all-reduce | flops 1536 | bytes 12288 | tf_op jit(solution)/shard_map/psum | solution.py:244
  727.2 63.1 %reduce-scatter.34.cloned.1.call-done = f32[96,512]{1,0:T(8,128)} async-done(((f32[768,512]{1,0:T(8,128)}), f32[96,512]{1,0:T(8,128)}) %reduce-scatter.34.cloned.1.call-update) | async-done | bytes 196624
  790.3 68.1 %reduce-scatter.30.cloned.1.call-done = f32[96,512]{1,0:T(8,128)} async-done(((f32[768,512]{1,0:T(8,128)}), f32[96,512]{1,0:T(8,128)}) %reduce-scatter.30.cloned.1.call-update) | async-done | bytes 196624 | tf_op jit(solution)/shard_map/reduce_scatter | solution.py:250
  858.3 67.8 %reduce-scatter.32.cloned.1.call-done = f32[96,512]{1,0:T(8,128)} async-done(((f32[768,512]{1,0:T(8,128)}), f32[96,512]{1,0:T(8,128)}) %reduce-scatter.32.cloned.1.call-update) | async-done | bytes 196624 | tf_op jit(solution)/shard_map/reduce_scatter | solution.py:251
  926.1 65.4 %reduce-scatter.28.cloned.1.call-done = f32[96,192]{1,0:T(8,128)} async-done(((f32[768,192]{1,0:T(8,128)}), f32[96,192]{1,0:T(8,128)}) %reduce-scatter.28.cloned.1.call-update) | async-done | bytes 73744 | tf_op jit(solution)/shard_map/reduce_scatter | solution.py:249
  991.5 65.4 %reduce-scatter.22.cloned.1.call-done = f32[96,192]{1,0:T(8,128)} async-done(((f32[768,192]{1,0:T(8,128)}), f32[96,192]{1,0:T(8,128)}) %reduce-scatter.22.cloned.1.call-update) | async-done | bytes 73744 | tf_op jit(solution)/shard_map/reduce_scatter | solution.py:246
  1056.9 65.5 %reduce-scatter.24.cloned.1.call-done = f32[96,192]{1,0:T(8,128)} async-done(((f32[768,192]{1,0:T(8,128)}), f32[96,192]{1,0:T(8,128)}) %reduce-scatter.24.cloned.1.call-update) | async-done | bytes 73744 | tf_op jit(solution)/shard_map/reduce_scatter | solution.py:247
  1122.4 65.2 %reduce-scatter.26.cloned.1.call-done = f32[96,192]{1,0:T(8,128)} async-done(((f32[768,192]{1,0:T(8,128)}), f32[96,192]{1,0:T(8,128)}) %reduce-scatter.26.cloned.1.call-update) | async-done | bytes 73744 | tf_op jit(solution)/shard_map/reduce_scatter | solution.py:248
  (320 shorter events, 252.9 us)
Async XLA Ops:
  7.2 68.4 %copy-start.42 = (bf16[96,192]{1,0:T(8,128)(2,1)S(1)}, bf16[96,192]{1,0:T(8,128)(2,1)}, u32[]{:S(2)}) copy-start(bf16[96,192]{1,0:T(8,128)(2,1)} %param.20) | copy-start | bytes 110596
  7.2 99.5 %copy-start.43 = (bf16[96,192]{1,0:T(8,128)(2,1)S(1)}, bf16[96,192]{1,0:T(8,128)(2,1)}, u32[]{:S(2)}) copy-start(bf16[96,192]{1,0:T(8,128)(2,1)} %param.21) | copy-start | bytes 110596
  7.2 130.5 %all-gather.5.cloned.1.call-start = ((), (), s32[]{:S(2)}) async-start(), calls=%async_computation.11 | async-start | bytes 3932160 | tf_op jit(solution)/shard_map/all_gather | solution.py:158
  11.5 281.9 %reduce-scatter.14.cloned.1.call-start = ((), (), s32[]{:S(2)}) async-start(), calls=%async_computation.12 | async-start | bytes 3932160 | tf_op jit(solution)/shard_map/reduce_scatter | solution.py:173
  44.7 96.7 %copy-start.23 = (bf16[768,192]{1,0:T(8,128)(2,1)}, bf16[768,192]{1,0:T(8,128)(2,1)S(1)}, u32[]{:S(2)}) copy-start(bf16[768,192]{1,0:T(8,128)(2,1)S(1)} %all_gather.34) | copy-start | bytes 884740
  75.6 69.1 %copy-start.25 = (bf16[768,192]{1,0:T(8,128)(2,1)}, bf16[768,192]{1,0:T(8,128)(2,1)S(1)}, u32[]{:S(2)}) copy-start(bf16[768,192]{1,0:T(8,128)(2,1)S(1)} %all_gather.35) | copy-start | bytes 884740
  251.5 42.0 %copy-start.4 = (bf16[512,768]{1,0:T(8,128)(2,1)S(1)}, bf16[512,768]{1,0:T(8,128)(2,1)}, u32[]{:S(2)}) copy-start(bf16[512,768]{1,0:T(8,128)(2,1)} %param.17) | copy-start | bytes 2359300
  254.2 41.3 %copy-start.36 = (f32[768]{0:T(1024)S(1)}, f32[768]{0:T(1024)}, u32[]{:S(2)}) copy-start(f32[768]{0:T(1024)} %param.26) | copy-start | bytes 9220
  254.3 145.3 %all-gather.7.cloned.1.call-start = ((), (), s32[]{:S(2)}) async-start(), calls=%async_computation.13 | async-start | bytes 3932160 | tf_op jit(solution)/shard_map/all_gather | solution.py:179
  254.3 44.1 %copy-start.35 = (bf16[96,512]{1,0:T(8,128)(2,1)S(1)}, bf16[96,512]{1,0:T(8,128)(2,1)}, u32[]{:S(2)}) copy-start(bf16[96,512]{1,0:T(8,128)(2,1)} %param.22) | copy-start | bytes 294916
  295.5 169.3 %copy-start.38 = (f32[512]{0:T(512)}, f32[512]{0:T(512)S(1)}, u32[]{:S(2)}) copy-start(f32[512]{0:T(512)S(1)} %get-tuple-element.380) | copy-start | bytes 6148
  297.8 111.5 %all-gather.9.cloned.1.call-start = ((), (), s32[]{:S(2)}) async-start(), calls=%async_computation.15 | async-start | bytes 3932160 | tf_op jit(solution)/shard_map/all_gather | solution.py:187
  298.4 163.9 %reduce-scatter.18.cloned.1.call-start = ((), (), s32[]{:S(2)}) async-start(), calls=%async_computation.16 | async-start | bytes 3932160 | tf_op jit(solution)/shard_map/reduce_scatter | solution.py:197
  424.2 38.1 %copy-start.9 = (bf16[512,768]{1,0:T(8,128)(2,1)S(1)}, bf16[512,768]{1,0:T(8,128)(2,1)}, u32[]{:S(2)}) copy-start(bf16[512,768]{1,0:T(8,128)(2,1)} %reduce-scatter.14.cloned.1.call-done) | copy-start | bytes 2359300
  424.2 72.7 %all-gather.11.cloned.1.call-start = ((), (), s32[]{:S(2)}) async-start(), calls=%async_computation.17 | async-start | bytes 3932160 | tf_op jit(solution)/shard_map/all_gather | solution.py:209
  468.2 213.9 %reduce-scatter.20.cloned.1.call-start = ((), (), s32[]{:S(2)}) async-start(), calls=%async_computation.18 | async-start | bytes 3932160 | tf_op jit(solution)/shard_map/reduce_scatter | solution.py:230
  642.2 81.6 %reduce-scatter.16.cloned.1.call-start = ((), (), s32[]{:S(2)}) async-start(), calls=%async_computation.14 | async-start | bytes 3932160 | tf_op jit(solution)/shard_map/reduce_scatter | solution.py:183
  647.6 142.7 %reduce-scatter.34.cloned.1.call-start = ((), (), s32[]{:S(2)}) async-start(), calls=%async_computation.25 | async-start | bytes 1769472
  657.7 200.6 %reduce-scatter.30.cloned.1.call-start = ((), (), s32[]{:S(2)}) async-start(), calls=%async_computation.23 | async-start | bytes 1769472 | tf_op jit(solution)/shard_map/reduce_scatter | solution.py:250
  662.4 263.8 %reduce-scatter.32.cloned.1.call-start = ((), (), s32[]{:S(2)}) async-start(), calls=%async_computation.24 | async-start | bytes 1769472 | tf_op jit(solution)/shard_map/reduce_scatter | solution.py:251
  667.0 324.5 %reduce-scatter.28.cloned.1.call-start = ((), (), s32[]{:S(2)}) async-start(), calls=%async_computation.22 | async-start | bytes 884736 | tf_op jit(solution)/shard_map/reduce_scatter | solution.py:249
  671.3 385.6 %reduce-scatter.22.cloned.1.call-start = ((), (), s32[]{:S(2)}) async-start(), calls=%async_computation.19 | async-start | bytes 884736 | tf_op jit(solution)/shard_map/reduce_scatter | solution.py:246
  674.4 448.0 %reduce-scatter.24.cloned.1.call-start = ((), (), s32[]{:S(2)}) async-start(), calls=%async_computation.20 | async-start | bytes 884736 | tf_op jit(solution)/shard_map/reduce_scatter | solution.py:247
  677.8 46.0 %copy-start.10 = (bf16[512,768]{1,0:T(8,128)(2,1)S(1)}, bf16[512,768]{1,0:T(8,128)(2,1)}, u32[]{:S(2)}) copy-start(bf16[512,768]{1,0:T(8,128)(2,1)} %reduce-scatter.14.cloned.1.call-done) | copy-start | bytes 2359300
  677.8 46.0 %copy-start.19 = (bf16[512,768]{1,0:T(8,128)(2,1)S(1)}, bf16[512,768]{1,0:T(8,128)(2,1)}, u32[]{:S(2)}) copy-start(bf16[512,768]{1,0:T(8,128)(2,1)} %param.29) | copy-start | bytes 2359300
  677.8 46.0 %copy-start.20 = (bf16[512,768]{1,0:T(8,128)(2,1)S(1)}, bf16[512,768]{1,0:T(8,128)(2,1)}, u32[]{:S(2)}) copy-start(bf16[512,768]{1,0:T(8,128)(2,1)} %reduce-scatter.18.cloned.1.call-done) | copy-start | bytes 2359300
  677.8 46.0 %copy-start.37 = (f32[768]{0:T(1024)S(1)}, f32[768]{0:T(1024)}, u32[]{:S(2)}) copy-start(f32[768]{0:T(1024)} %param.26) | copy-start | bytes 9220
  677.8 46.0 %copy-start.39 = (f32[512]{0:T(512)S(1)}, f32[512]{0:T(512)}, u32[]{:S(2)}) copy-start(f32[512]{0:T(512)} %copy-done.38) | copy-start | bytes 6148
  677.8 46.0 %copy-start.47 = (f32[512]{0:T(512)S(1)}, f32[512]{0:T(512)}, u32[]{:S(2)}) copy-start(f32[512]{0:T(512)} %get-tuple-element.379) | copy-start | bytes 6148
  677.9 46.0 %copy-start.49 = (f32[512]{0:T(512)S(1)}, f32[512]{0:T(512)}, u32[]{:S(2)}) copy-start(f32[512]{0:T(512)} %copy-done.48) | copy-start | bytes 6148
  677.9 46.0 %copy-start.51 = (f32[512]{0:T(512)S(1)}, f32[512]{0:T(512)}, u32[]{:S(2)}) copy-start(f32[512]{0:T(512)} %get-tuple-element.377) | copy-start | bytes 6148
  677.9 509.8 %reduce-scatter.26.cloned.1.call-start = ((), (), s32[]{:S(2)}) async-start(), calls=%async_computation.21 | async-start | bytes 884736 | tf_op jit(solution)/shard_map/reduce_scatter | solution.py:248
  (61 other events, 353.9 us)
Sparse Core Ops, SparseCore 0:
  11.6 31.2 all-gather.4
  254.4 39.0 reduce-scatter.13
  297.9 28.5 all-gather.6
  328.0 28.5 all-gather.8
  424.3 37.9 reduce-scatter.17
  468.4 28.5 all-gather.10
  642.4 37.9 reduce-scatter.19
  683.0 38.1 reduce-scatter.15
  725.3 64.9 reduce-scatter.33
  794.5 63.7 reduce-scatter.29
  862.3 63.7 reduce-scatter.31
  930.2 61.2 reduce-scatter.27
  995.4 61.4 reduce-scatter.21
  1061.0 61.3 reduce-scatter.23
  1126.2 61.4 reduce-scatter.25
where the time goes:
time: 1200 us; the launch traced here: 1190 us
  waiting for transfers between devices  567 us (47%)
  blocking collectives  267 us (22%)
  matrix products  213 us (18%)
  other arithmetic  96.7 us (8%)
  local copies, waits for them, and re-layouts  28.2 us (2%)
  between operations  14.8 us (1%)
    reduce_scatter x1, waiting for transfers between devices, local(): lax.psum_scatter(grad_gate, 'dp', scatter_dimension=0, tiled=True)  68.1 us
    reduce_scatter x1, waiting for transfers between devices, local(): lax.psum_scatter(grad_up, 'dp', scatter_dimension=0, tiled=True)  67.8 us
    reduce_scatter x1, waiting for transfers between devices, local(): lax.psum_scatter(grad_key, 'dp', scatter_dimension=0, tiled=True)  65.5 us
    reduce_scatter x1, waiting for transfers between devices, local(): lax.psum_scatter(grad_out, 'dp', scatter_dimension=0, tiled=True)  65.4 us
    reduce_scatter x1, waiting for transfers between devices, local(): lax.psum_scatter(grad_query, 'dp', scatter_dimension=0, tiled=True)  65.4 us
    reduce_scatter x1, waiting for transfers between devices, local(): lax.psum_scatter(grad_value, 'dp', scatter_dimension=0, tiled=True)  65.2 us
    unnamed x16, waiting for transfers between devices  63.9 us
    psum x1, blocking collectives, local(): lax.psum((gain_attn_part, gain_mlp_part), ('dp', 'mp'))  39.8 us
  transfers between devices with their start and end apart: 15, of which 10 were waited for; matrix products, arithmetic and copies ran while one was open for 4% of the time, Pallas kernels for 0%

commit v1 on v0

v1 whole, which is shorter than its diff:
```python
import functools

import jax
import jax.numpy as jnp
from jax import lax
from jax.experimental import pallas as pl
from jax.experimental.pallas import tpu as pltpu
from jax.sharding import PartitionSpec as P

HEAD = 64
BLK = 256
DIRECT = 8
eps_norm = 1e-06
neg_large = -1e30
F32 = jnp.float32
BF16 = jnp.bfloat16


def nn(a, b):
    return lax.dot_general(a, b, (((1,), (0,)), ((), ())), preferred_element_type=F32)


def nt(a, b):
    return lax.dot_general(a, b, (((1,), (1,)), ((), ())), preferred_element_type=F32)


def tn(a, b):
    return lax.dot_general(a, b, (((0,), (0,)), ((), ())), preferred_element_type=F32)


def shape(dims, kind):
    return jax.ShapeDtypeStruct(dims, kind)


def whole(dims):
    return pl.BlockSpec(dims, lambda *_: (0,) * len(dims))


SMEM = pl.BlockSpec(memory_space=pltpu.SMEM)


def qkv_kernel(pieces, sc, t0, t1, t2, t3, gain, *rest):
    w_refs, (n1_o, qkvt_o, kn_o, vn_o, wt_o, xs, ws) = rest[:pieces], rest[pieces:]
    step = pl.program_id(0)
    cols = kn_o.shape[1]

    @pl.when(step == 0)
    def _():
        if pieces == 1:
            ws[...] = w_refs[0][...]
        else:
            depth = w_refs[0].shape[0]
            for j in range(pieces):
                at = pl.multiple_of((sc[1] ^ j) * depth, 16)
                ws[pl.ds(at, depth), :] = w_refs[j][...]
        wt_o[...] = ws[...].T

    for j, ref in enumerate((t0, t1, t2, t3)):

        @pl.when(step == j)
        def _(ref=ref):
            xs[...] = ref[...]

    x = xs[...].astype(F32)
    scale = lax.rsqrt(jnp.mean(x * x, axis=-1, keepdims=True) + eps_norm)
    n1 = (x * scale * gain[...]).astype(BF16)
    n1_o[...] = n1
    qkvt_o[...] = nt(wt_o[0 : 3 * cols, :], n1).astype(BF16)
    kn_o[...] = nn(n1, ws[:, 0:cols]).astype(BF16)
    vn_o[...] = nn(n1, ws[:, 2 * cols : 3 * cols]).astype(BF16)


def qkv(sc, shards, gain, pieces, cols):
    rows, width = shards[0].shape
    total = rows * len(shards)
    return pl.pallas_call(
        functools.partial(qkv_kernel, len(pieces)),
        grid=(len(shards),),
        in_specs=[SMEM]
        + [whole((rows, width))] * 4
        + [whole((1, width))]
        + [whole(p.shape) for p in pieces],
        out_specs=[
            pl.BlockSpec((rows, width), lambda i: (i, 0)),
            pl.BlockSpec((3 * cols, rows), lambda i: (0, i)),
            pl.BlockSpec((rows, cols), lambda i: (i, 0)),
            pl.BlockSpec((rows, cols), lambda i: (i, 0)),
            whole((4 * cols, width)),
        ],
        out_shape=[
            shape((total, width), BF16),
            shape((3 * cols, total), BF16),
            shape((total, cols), BF16),
            shape((total, cols), BF16),
            shape((4 * cols, width), BF16),
        ],
        scratch_shapes=[pltpu.VMEM((rows, width), BF16), pltpu.VMEM((width, 4 * cols), BF16)],
        name="qkv",
    )(sc, *shards, gain, *pieces)


def spread(rows, z_ref):
    heads = rows.shape[0] // HEAD
    z_ref[...] = jnp.zeros(z_ref.shape, z_ref.dtype)
    for h in range(heads):
        z_ref[h, h * HEAD : (h + 1) * HEAD, :] = rows[h * HEAD : (h + 1) * HEAD, :]


def placed(block, me, per):
    return ((block // per) ^ me) * per + lax.rem(block, per)


def span(sc, half, per, blocks):
    me = sc[0]
    stored = half * blocks + pl.program_id(0)
    place = placed(stored, me, per)
    low, high = sc[8 + place], sc[16 + place]
    has_own = jnp.logical_and(low <= place, place < high)
    count = jnp.maximum(high - low, 0) - has_own.astype(jnp.int32)

    def at(t):
        block = low + t
        block = block + (block >= place).astype(jnp.int32)
        return placed(block, me, per)

    return stored, count, at


def allowed(gkv, gq, start, own):
    keys = gkv[pl.ds(start, BLK), :]
    mask = jnp.concatenate([keys] * (BLK // 128), axis=1) == gq[...]
    if own:
        mask = mask | (
            lax.broadcasted_iota(jnp.int32, (BLK, BLK), 0)
            == lax.broadcasted_iota(jnp.int32, (BLK, BLK), 1)
        )
    return mask


def forward_kernel(half, per, sc, qt, kn, vt, gq, gkv, ot, lse, zq):
    heads = qt.shape[0] // HEAD
    stored, count, at = span(sc, half, per, pl.num_programs(0))
    spread(qt, zq)

    def scores(start, own):
        mask = allowed(gkv, gq, start, own)
        keys = kn[pl.ds(start, BLK), :]
        return [jnp.where(mask, nn(keys, zq[h]), neg_large) for h in range(heads)]

    def mixed(h, start, p):
        return nn(vt[h * HEAD : (h + 1) * HEAD, pl.ds(start, BLK)], p.astype(BF16))

    start = pl.multiple_of(stored * BLK, BLK)
    carry = []
    for h, s in enumerate(scores(start, True)):
        top = jnp.max(s, axis=0, keepdims=True)
        p = jnp.exp(s - top)
        carry.append((top, jnp.sum(p, axis=0, keepdims=True), mixed(h, start, p)))

    def body(t, carry):
        start = pl.multiple_of(at(t) * BLK, BLK)
        out = []
        for h, s in enumerate(scores(start, False)):
            top, total, acc = carry[h]
            higher = jnp.maximum(top, jnp.max(s, axis=0, keepdims=True))
            p = jnp.exp(s - higher)
            fade = jnp.exp(top - higher)
            out.append(
                (
                    higher,
                    fade * total + jnp.sum(p, axis=0, keepdims=True),
                    fade * acc + mixed(h, start, p),
                )
            )
        return tuple(out)

    carry = lax.fori_loop(0, count, body, tuple(carry))
    for h, (top, total, acc) in enumerate(carry):
        ot[h * HEAD : (h + 1) * HEAD, :] = (acc / total).astype(BF16)
        lse[h : h + 1, :] = top + jnp.log(total)


def attention(half, sc, qkvt, kn, gq, gkv):
    cols3, total = qkvt.shape
    cols = cols3 // 3
    blocks = total // BLK // 2
    per = total // 4 // BLK
    return pl.pallas_call(
        functools.partial(forward_kernel, half, per),
        grid=(blocks,),
        in_specs=[
            SMEM,
            pl.BlockSpec((cols, BLK), lambda i: (1, half * blocks + i)),
            whole((total, cols)),
            pl.BlockSpec((cols, total), lambda i: (2, 0)),
            pl.BlockSpec((1, BLK), lambda i: (0, half * blocks + i)),
            whole((total, 128)),
        ],
        out_specs=[
            pl.BlockSpec((cols, BLK), lambda i: (0, i)),
            pl.BlockSpec((8, BLK), lambda i: (0, i)),
        ],
        out_shape=[shape((cols, blocks * BLK), BF16), shape((8, blocks * BLK), F32)],
        scratch_shapes=[pltpu.VMEM((cols // HEAD, cols, BLK), BF16)],
        name="attention",
    )(sc, qkvt, kn, qkvt, gq, gkv)


def backward_kernel(
    half, per, first, sc, qt, kn, kt, vn, dot_, ot, lse, gq, gkv, *rest
):
    if first:
        dqt, dk_o, dv_o, dk, dv, zq, zd = rest
    else:
        dk_i, dv_i, dqt, dk_o, dv_o, dk, dv, zq, zd = rest
    heads = qt.shape[0] // HEAD
    step = pl.program_id(0)
    stored, count, at = span(sc, half, per, pl.num_programs(0))

    @pl.when(step == 0)
    def _():
        if first:
            dk[...] = jnp.zeros(dk.shape, F32)
            dv[...] = jnp.zeros(dv.shape, F32)
        else:
            dk[...] = dk_i[...]
            dv[...] = dv_i[...]

    spread(qt, zq)
    spread(dot_, zd)
    deltas = []
    for h in range(heads):
        part = slice(h * HEAD, (h + 1) * HEAD)
        deltas.append(
            jnp.sum(dot_[part, :].astype(F32) * ot[part, :].astype(F32), axis=0, keepdims=True)
        )

    def one(start, own):
        mask = allowed(gkv, gq, start, own)
        keys, values = kn[pl.ds(start, BLK), :], vn[pl.ds(start, BLK), :]
        out = []
        for h in range(heads):
            part = slice(h * HEAD, (h + 1) * HEAD)
            s = jnp.where(mask, nn(keys, zq[h]), neg_large)
            p = jnp.exp(s - lse[h : h + 1, :])
            ds = (p * (nn(values, zd[h]) - deltas[h])).astype(BF16)
            at_keys = pl.ds(start, BLK)
            dv[part, at_keys] += nt(dot_[part, :], p.astype(BF16))
            dk[part, at_keys] += nt(qt[part, :], ds)
            out.append(nn(kt[part, at_keys], ds))
        return out

    carry = one(pl.multiple_of(stored * BLK, BLK), True)

    def body(t, carry):
        new = one(pl.multiple_of(at(t) * BLK, BLK), False)
        return tuple(c + n for c, n in zip(carry, new))

    carry = lax.fori_loop(0, count, body, tuple(carry))
    for h in range(heads):
        dqt[h * HEAD : (h + 1) * HEAD, :] = carry[h].astype(BF16)

    @pl.when(step == pl.num_programs(0) - 1)
    def _():
        dk_o[...] = dk[...].astype(dk_o.dtype)
        dv_o[...] = dv[...].astype(dv_o.dtype)


def attention_back(half, first, sc, qkvt, kn, vn, dout, out, lse, gq, gkv, sums=()):
    cols3, total = qkvt.shape
    cols = cols3 // 3
    blocks = total // BLK // 2
    per = total // 4 // BLK
    kind = F32 if first else BF16
    return pl.pallas_call(
        functools.partial(backward_kernel, half, per, first),
        grid=(blocks,),
        in_specs=[
            SMEM,
            pl.BlockSpec((cols, BLK), lambda i: (1, half * blocks + i)),
            whole((total, cols)),
            pl.BlockSpec((cols, total), lambda i: (0, 0)),
            whole((total, cols)),
            pl.BlockSpec((cols, BLK), lambda i: (0, i)),
            pl.BlockSpec((cols, BLK), lambda i: (0, i)),
            pl.BlockSpec((8, BLK), lambda i: (0, i)),
            pl.BlockSpec((1, BLK), lambda i: (0, half * blocks + i)),
            whole((total, 128)),
        ]
        + [whole((cols, total))] * len(sums),
        out_specs=[
            pl.BlockSpec((cols, BLK), lambda i: (0, i)),
            whole((cols, total)),
            whole((cols, total)),
        ],
        out_shape=[
            shape((cols, blocks * BLK), BF16),
            shape((cols, total), kind),
            shape((cols, total), kind),
        ],
        scratch_shapes=[
            pltpu.VMEM((cols, total), F32),
            pltpu.VMEM((cols, total), F32),
            pltpu.VMEM((cols // HEAD, cols, BLK), BF16),
            pltpu.VMEM((cols // HEAD, cols, BLK), BF16),
        ],
        name="attention_back",
    )(sc, qkvt, kn, qkvt, vn, dout, out, lse, gq, gkv, *sums)


def out_kernel(om, ox, wm, wx, own, other):
    rows = own.shape[0]
    part = nn(om[...].T, wm[...]) + nn(ox[...].T, wx[...])
    own[...] = part[:rows]
    other[...] = part[rows:].astype(BF16)


def out_projection(om, ox, wm, wx):
    cols, both = om.shape
    width = wm.shape[1]
    return pl.pallas_call(
        out_kernel,
        out_shape=[shape((both // 2, width), F32), shape((both // 2, width), BF16)],
        name="out_projection",
    )(om, ox, wm, wx)


def middle_kernel(tokens, own, got, gain, h1_o, n2_o):
    h1 = tokens[...].astype(F32) + (own[...] + got[...].astype(F32))
    scale = lax.rsqrt(jnp.mean(h1 * h1, axis=-1, keepdims=True) + eps_norm)
    h1_o[...] = h1
    n2_o[...] = (h1 * scale * gain[...]).astype(BF16)


def middle(tokens, own, got, gain):
    rows, width = tokens.shape
    tile = pl.BlockSpec((rows // 4, width), lambda i: (i, 0))
    return pl.pallas_call(
        middle_kernel,
        grid=(4,),
        in_specs=[tile, tile, tile, whole((1, width))],
        out_specs=[tile, tile],
        out_shape=[shape((rows, width), F32), shape((rows, width), BF16)],
        name="middle",
    )(tokens, own, got, gain)


def mlp_kernel(na, nb, ya, yb, wg, wu, wd, ma, mb, da, db, hid_o, dgu_o):
    step = pl.program_id(0)
    lower = step < pl.num_programs(0) // 2
    n2 = jnp.where(lower, na[...], nb[...])
    dy = jnp.where(lower, ya[...], yb[...])
    gate, up = nn(n2, wg[...]), nn(n2, wu[...])
    inner = 0.7978845608028654 * (gate + 0.044715 * gate * gate * gate)
    t = jnp.tanh(inner)
    value = 0.5 * gate * (1.0 + t)
    hidden = (value * up).astype(BF16)
    hid_o[...] = hidden
    dhid = nn(dy, wd[...])
    slope = 0.5 * (1.0 + t) + 0.5 * gate * (1.0 - t * t) * 0.7978845608028654 * (
        1.0 + 3.0 * 0.044715 * gate * gate
    )
    units = wg.shape[1]
    dgate = (dhid * up * slope).astype(BF16)
    dup = (dhid * value).astype(BF16)
    dgu_o[:, 0:units] = dgate
    dgu_o[:, units : 2 * units] = dup
    dn2 = (nt(dgate, wg[...]) + nt(dup, wu[...])).astype(BF16)
    mlp = nt(hidden, wd[...]).astype(BF16)

    @pl.when(lower)
    def _():
        da[...] = dn2
        ma[...] = mlp

    @pl.when(jnp.logical_not(lower))
    def _():
        db[...] = dn2
        mb[...] = mlp


def mlp_both(na, nb, ya, yb, weights):
    rows, width = na.shape
    units = weights.shape[1] // 3
    tile = 256
    per = rows // tile
    first = pl.BlockSpec((tile, width), lambda i: (jnp.minimum(i, per - 1), 0))
    second = pl.BlockSpec((tile, width), lambda i: (jnp.maximum(i - per, 0), 0))
    part = [pl.BlockSpec((width, units), functools.partial(lambda j, i: (0, j), j)) for j in range(3)]
    return pl.pallas_call(
        mlp_kernel,
        grid=(2 * per,),
        in_specs=[first, second, first, second, *part],
        out_specs=[
            first,
            second,
            first,
            second,
            pl.BlockSpec((tile, units), lambda i: (i, 0)),
            pl.BlockSpec((tile, 2 * units), lambda i: (i, 0)),
        ],
        out_shape=[shape((rows, width), BF16)] * 4
        + [shape((2 * rows, units), BF16), shape((2 * rows, 2 * units), BF16)],
        name="mlp",
    )(na, nb, ya, yb, weights, weights, weights)


def middle_back_kernel(dy, h1_r, a, b, c, gain, dh1_o, da_o, gain_o):
    dn2 = a[...].astype(F32) + b[...].astype(F32) + c[...].astype(F32)
    h1 = h1_r[...]
    scale = lax.rsqrt(jnp.mean(h1 * h1, axis=-1, keepdims=True) + eps_norm)
    hat = dn2 * gain[...]
    dh1 = (
        dy[...].astype(F32)
        + scale * hat
        - h1 * (scale * scale * scale) * jnp.mean(hat * h1, axis=-1, keepdims=True)
    )
    dh1_o[...] = dh1
    da_o[...] = dh1.astype(BF16)

    @pl.when(pl.program_id(0) == 0)
    def _():
        gain_o[...] = jnp.zeros(gain_o.shape, F32)

    gain_o[...] += jnp.sum(dn2 * h1 * scale, axis=0, keepdims=True)


def middle_back(dy, h1, a, b, c, gain):
    rows, width = h1.shape
    tile = pl.BlockSpec((rows // 4, width), lambda i: (i, 0))
    return pl.pallas_call(
        middle_back_kernel,
        grid=(4,),
        in_specs=[tile] * 5 + [whole((1, width))],
        out_specs=[tile, tile, whole((1, width))],
        out_shape=[shape((rows, width), F32), shape((rows, width), BF16), shape((1, width), F32)],
        name="middle_back",
    )(dy, h1, a, b, c, gain)


def out_back_kernel(own, other, wm, wx, om, ox, dm_o, dx_o, gm_o, gx_o):
    rows = own.shape[0]
    for at, ref in ((0, own), (rows, other)):
        dm_o[:, at : at + rows] = nt(wm[...], ref[...]).astype(BF16)
        dx_o[:, at : at + rows] = nt(wx[...], ref[...]).astype(BF16)
    gm_o[...] = nn(om[:, :rows], own[...]) + nn(om[:, rows:], other[...])
    gx_o[...] = (nn(ox[:, :rows], own[...]) + nn(ox[:, rows:], other[...])).astype(BF16)


def out_back(own, other, wm, wx, om, ox):
    cols, both = om.shape
    width = own.shape[1]
    return pl.pallas_call(
        out_back_kernel,
        out_shape=[
            shape((cols, both), BF16),
            shape((cols, both), BF16),
            shape((cols, width), F32),
            shape((cols, width), BF16),
        ],
        name="out_back",
    )(own, other, wm, wx, om, ox)


def rows_back_kernel(dk, dq, dv, wt, a_o, b_o):
    rows = a_o.shape[0]
    grads = jnp.concatenate([dk[...], dq[...], dv[...]], axis=0)
    part = nn(grads.T, wt[0 : grads.shape[0], :]).astype(BF16)
    a_o[...] = part[:rows]
    b_o[...] = part[rows:]


def rows_back(half, dk, dq, dv, wt):
    cols, both = dq.shape
    width = wt.shape[1]
    side = pl.BlockSpec((cols, both), lambda i: (0, half))
    return pl.pallas_call(
        rows_back_kernel,
        grid=(1,),
        in_specs=[side, whole((cols, both)), side, whole(wt.shape)],
        out_specs=[whole((both // 2, width))] * 2,
        out_shape=[shape((both // 2, width), BF16)] * 2,
        name="rows_back",
    )(dk, dq, dv, wt)


def weights_back_kernel(pieces, sc, dk, dqa, dqb, dv, n1, wt, gain, gain_o, *rest):
    outs, gs = rest[:pieces], rest[pieces]
    cols, half = dqa.shape
    gt = [
        nn(dk[...], n1[...]),
        nn(dqa[...], n1[:half, :]) + nn(dqb[...], n1[half:, :]),
        nn(dv[...], n1[...]),
    ]
    total = jnp.zeros(gain.shape, F32)
    for j in range(3):
        at = slice(j * cols, (j + 1) * cols)
        total += jnp.sum(gt[j] * wt[at, :].astype(F32), axis=0, keepdims=True)
    gain_o[...] = total / gain[...]
    gs[...] = jnp.concatenate(gt, axis=0).T.astype(BF16)
    if pieces == 1:
        outs[0][...] = gs[...]
    else:
        depth = outs[0].shape[0]
        for j in range(pieces):
            outs[j][...] = gs[pl.ds(pl.multiple_of((sc[1] ^ j) * depth, 16), depth), :]


def weights_back(pieces, sc, dk, dqa, dqb, dv, n1, wt, gain):
    cols, total = dk.shape
    width = n1.shape[1]
    return pl.pallas_call(
        functools.partial(weights_back_kernel, pieces),
        in_specs=[SMEM] + [pl.BlockSpec(memory_space=pltpu.VMEM)] * 7,
        out_shape=[shape((1, width), F32)]
        + [shape((width // pieces, 3 * cols), BF16)] * pieces,
        scratch_shapes=[pltpu.VMEM((width, 3 * cols), BF16)],
        name="weights_back",
    )(sc, dk, dqa, dqb, dv, n1, wt, gain)


def last_kernel(tokens, dh1, a, b, c, gain, out):
    x = tokens[...].astype(F32)
    dn1 = a[...].astype(F32) + b[...].astype(F32) + c[...].astype(F32)
    scale = lax.rsqrt(jnp.mean(x * x, axis=-1, keepdims=True) + eps_norm)
    hat = dn1 * gain[...]
    out[...] = (
        dh1[...]
        + scale * hat
        - x * (scale * scale * scale) * jnp.mean(hat * x, axis=-1, keepdims=True)
    ).astype(BF16)


def last(tokens, dh1, a, b, c, gain):
    rows, width = tokens.shape
    tile = pl.BlockSpec((rows // 4, width), lambda i: (i, 0))
    return pl.pallas_call(
        last_kernel,
        grid=(4,),
        in_specs=[tile] * 5 + [whole((1, width))],
        out_specs=tile,
        out_shape=shape((rows, width), BF16),
        name="last",
    )(tokens, dh1, a, b, c, gain)


def local(
    dp,
    mp,
    tokens,
    w_query,
    w_key,
    w_value,
    w_out,
    w_gate,
    w_up,
    w_down,
    norm_attn,
    norm_mlp,
    valid_counts,
    group_ids,
    cotangent,
):
    me, row = lax.axis_index("mp"), lax.axis_index("dp")
    cols = w_query.shape[1]
    length = group_ids.shape[1]

    def core(v):
        return lax.ppermute(v, "mp", [(i, i ^ 1) for i in range(mp)])

    def across(v):
        return lax.ppermute(v, "mp", [(i, i ^ 2) for i in range(mp)])

    def far(v, k):
        return lax.ppermute(v, "dp", [(i, i ^ k) for i in range(dp)])

    def after(v, *others):
        return lax.optimization_barrier((v, *others))[0]

    direct = dp <= DIRECT
    gain_a, gain_m = norm_attn[None], norm_mlp[None]

    tok2 = across(tokens)
    tok1 = core(tokens)
    w_attn = jnp.concatenate([w_key, w_query, w_value, w_out], axis=1)
    if direct:
        w_pieces = [w_attn] + [far(w_attn, k) for k in range(1, dp)]
    else:
        w_pieces = [lax.all_gather(w_attn, "dp", axis=0, tiled=True)]
    w_mlp = lax.all_gather(
        jnp.concatenate([w_gate, w_up, w_down], axis=1), "dp", axis=0, tiled=True
    )
    tok3 = core(tok2)

    ids = group_ids.reshape(4, length // 4)
    valid = valid_counts[0]
    flat = ids.reshape(-1)
    tiles = flat.reshape(length // BLK, BLK)
    low = jnp.sum(flat[None, :] < tiles[:, :1], axis=1) // BLK
    high = jnp.minimum(jnp.sum(flat[None, :] <= tiles[:, -1:], axis=1), valid)
    high = (high + BLK - 1) // BLK
    head = jnp.stack([me, row, valid, valid, valid, valid, valid, valid])
    sc = jnp.concatenate([head, low, high]).astype(jnp.int32)
    place = jnp.arange(length, dtype=jnp.int32).reshape(4, length // 4)
    keyed = jnp.where(place < valid, ids, -1)

    def relative(v):
        v = jnp.where(me % 2 == 1, v[jnp.array([1, 0, 3, 2])], v)
        return jnp.where(me >= 2, v[jnp.array([2, 3, 0, 1])], v)

    gq = relative(ids).reshape(1, length)
    gkv = jnp.broadcast_to(relative(keyed).reshape(length, 1), (length, 128))

    n1, qkvt, kn, vn, wt = qkv(sc, (tokens, tok1, tok2, tok3), gain_a, w_pieces, cols)
    wo = wt[3 * cols :]
    wo_x = across(wo)
    dy0 = cotangent
    dy2 = across(after(cotangent, wo))
    dy1 = core(after(cotangent, wo))
    dy3 = core(dy2)

    o_far, lse_far = attention(1, sc, qkvt, kn, gq, gkv)
    o_x = across(o_far)
    o_own, lse_own = attention(0, after(sc, o_far), qkvt, kn, gq, gkv)
    p_own, p_other = out_projection(o_own, o_x, wo, wo_x)
    h1, n2 = middle(tokens, p_own, core(p_other), gain_m)

    n2_2 = across(n2)
    n2_1 = core(n2)
    n2_3 = core(n2_2)
    m0, m1, d0, d1, hid_a, dgu_a = mlp_both(n2, n2_1, dy0, dy1, w_mlp)
    m2, m3, d2, d3, hid_b, dgu_b = mlp_both(n2_2, n2_3, dy2, dy3, w_mlp)

    def summed(a, b):
        return (a.astype(F32) + b.astype(F32)).astype(BF16)

    d_x = across(summed(d2, core(d3)))
    dh1, da, gain_m_part = middle_back(dy0, h1, d0, core(d1), d_x, gain_m)
    m_x = across(summed(after(m2, d_x), core(after(m3, d_x))))
    output = (
        h1 + (m0.astype(F32) + core(m1).astype(F32) + m_x.astype(F32))
    ).astype(BF16)
    n2_a = jnp.concatenate([n2, n2_1], axis=0)
    n2_b = jnp.concatenate([n2_2, n2_3], axis=0)
    dy_a = jnp.concatenate([dy0, dy1], axis=0)
    dy_b = jnp.concatenate([dy2, dy3], axis=0)
    grad_gu = tn(n2_a, dgu_a) + tn(n2_b, dgu_b)
    grad_d = tn(dy_a, hid_a) + tn(dy_b, hid_b)

    do_own, do_send, go, go_send = out_back(da, core(da), wo, wo_x, o_own, o_x)
    do_far = across(do_send)
    grad_o = (go + across(go_send).astype(F32)).T
    mlp_grads = lax.psum_scatter(
        jnp.concatenate([grad_gu.astype(BF16), grad_d.astype(BF16), grad_o.astype(BF16)], axis=1),
        "dp",
        scatter_dimension=0,
        tiled=True,
    ).astype(F32)

    dq_own, dk, dv = attention_back(
        0, True, sc, qkvt, kn, vn, do_own, o_own, lse_own, gq, gkv
    )
    dq_far, dk, dv = attention_back(
        1, False, sc, qkvt, kn, vn, do_far, o_far, lse_far, gq, gkv, (dk, dv)
    )
    r2, r3 = rows_back(1, dk, dq_far, dv, wt)
    r_x = across(summed(r2, core(r3)))
    if direct:
        pieces = dp
    else:
        pieces = 1
    gain_a_part, *grads = weights_back(
        pieces, sc, after(dk, r2), dq_own, dq_far, dv, n1, wt, gain_a
    )
    if direct:
        attn_grads = grads[0].astype(F32)
        for k in range(1, dp):
            attn_grads = attn_grads + far(grads[k], k).astype(F32)
    else:
        attn_grads = lax.psum_scatter(
            grads[0], "dp", scatter_dimension=0, tiled=True
        ).astype(F32)
    r0, r1 = rows_back(0, dk, dq_own, dv, wt)
    grad_tokens = last(tokens, dh1, r0, core(r1), r_x, gain_a)

    gains = jnp.concatenate([gain_a_part, gain_m_part], axis=0)
    if direct:
        gains = gains + core(gains)
        gains = gains + across(gains)
        k = 1
        while k < dp:
            gains = gains + far(gains, k)
            k *= 2
    else:
        gains = lax.psum(gains, ("dp", "mp"))

    units = w_gate.shape[1]
    return (
        output,
        grad_tokens,
        attn_grads[:, cols : 2 * cols],
        attn_grads[:, :cols],
        attn_grads[:, 2 * cols :],
        mlp_grads[:, 3 * units :],
        mlp_grads[:, :units],
        mlp_grads[:, units : 2 * units],
        mlp_grads[:, 2 * units : 3 * units],
        gains[0],
        gains[1],
    )


def solution(mesh):
    rows, weight = P(("dp", "mp"), None), P("dp", "mp")
    return jax.shard_map(
        functools.partial(local, mesh.shape["dp"], mesh.shape["mp"]),
        mesh=mesh,
        in_specs=(rows,) + (weight,) * 7 + (P(), P(), P("dp"), P("dp", None), rows),
        out_specs=(rows, rows) + (weight,) * 7 + (P(), P()),
        check_vma=False,
    )
```

time: 1200 us -> 371 us (0.31)
  waiting for transfers between devices: 567 us -> 111 us
  blocking collectives: 267 us -> 0 us
  matrix products: 213 us -> 15.5 us
  Pallas kernels: 0 us -> 121 us
  other arithmetic: 96.7 us -> 13.7 us
  starting transfers between devices: 0.83 us -> 75.5 us
    reduce_scatter x10 -> x1, waiting for transfers between devices: 475 us -> 0.01 us  [local(): lax.psum_scatter(jnp.concatenate([grad_gu.astype(BF16), grad_d.astype(BF1...]
    all_gather x7 -> x0, blocking collectives: 227 us -> none  [the longest x1 34.3 us: local(): lax.all_gather(w_down, 'dp', axis=0, tiled=True)]
    dot_general x49 -> x4, matrix products: 213 us -> 15.5 us  [tn(): lax.dot_general(a, b, (((0,), (0,)), ((), ())), preferred_element_type=F32)]
    pallas_call x0 -> x15, Pallas kernels: none -> 121 us  [the longest x2 34.1 us: attention_back(): pl.pallas_call(functools.partial(backward_kernel, half, per, first), grid...]
    ppermute x0 -> x43, waiting for transfers between devices: none -> 111 us  [the longest x11 69.9 us: across(): return lax.ppermute(v, 'mp', [(i, i ^ 2) for i in range(mp)])]
    ppermute x0 -> x43, starting transfers between devices: none -> 75.4 us  [the longest x17 54.5 us: far(): return lax.ppermute(v, 'dp', [(i, i ^ k) for i in range(dp)])]
    unnamed x16 -> x2, waiting for transfers between devices: 63.9 us -> 0.03 us
    psum x1 -> x0, blocking collectives: 39.8 us -> none  [local(): lax.psum((gain_attn_part, gain_mlp_part), ('dp', 'mp'))]
  transfers between devices with their start and end apart: 15 -> 45, of which waited for: 10 -> 21; matrix products, arithmetic and copies ran while one was open for 4% -> 10% of each run, Pallas kernels for 0% -> 30%
where the time goes in v1:
time: 371 us; the launch traced here: 373 us
  Pallas kernels  121 us (33%)
  waiting for transfers between devices  111 us (30%)
  starting transfers between devices  75.5 us (20%)
  local copies, waits for them, and re-layouts  21.4 us (6%)
  matrix products  15.5 us (4%)
  between operations  15.2 us (4%)
  other arithmetic  13.7 us (4%)
    ppermute x11, waiting for transfers between devices, across(): return lax.ppermute(v, 'mp', [(i, i ^ 2) for i in range(mp)])  69.9 us
    ppermute x17, starting transfers between devices, far(): return lax.ppermute(v, 'dp', [(i, i ^ k) for i in range(dp)])  54.5 us
    ppermute x17, waiting for transfers between devices, far(): return lax.ppermute(v, 'dp', [(i, i ^ k) for i in range(dp)])  38.4 us
    pallas_call x2, Pallas kernels, attention_back(): pl.pallas_call(functools.partial(backward_kernel, half, per, first), grid...  34.1 us
    pallas_call x2, Pallas kernels, mlp_both(): pl.pallas_call(mlp_kernel, grid=(2 * per,), in_specs=[first, second, firs...  20.8 us
    pallas_call x2, Pallas kernels, attention(): pl.pallas_call(functools.partial(forward_kernel, half, per), grid=(blocks...  20.3 us
    ppermute x11, starting transfers between devices, across(): return lax.ppermute(v, 'mp', [(i, i ^ 2) for i in range(mp)])  18.5 us
    dot_general x4, matrix products, tn(): lax.dot_general(a, b, (((0,), (0,)), ((), ())), preferred_element_type=F32)  15.5 us
  transfers between devices with their start and end apart: 45, of which 21 were waited for; matrix products, arithmetic and copies ran while one was open for 10% of the time, Pallas kernels for 30%

profile of v1, /device:TPU:0, one launch (start us, length us, event | category | flops | bytes accessed | tf_op | source)
XLA Modules:
  0.0 372.9 jit_solution(17358814797342625343)
XLA Ops:
  23.6 5.1 %collective-permute-done.1.t2 = bf16[512,768]{1,0:T(8,128)(2,1)S(1)} collective-permute-done((bf16[512,768]{1,0:T(8,128)(2,1)}, bf16[512,768]{1,0:T(8,128)(2,1)S(1)}, u32[]{:S(2)}, u32[]{:S(2)}) %collective-permute-start.1) | collective-permute-done | bytes 786464 | tf_op jit(solution)/shard_map/ppermute | solution.py:572
  37.0 3.6 collective-permute-start.8
  40.6 11.4 %collective-permute-done.6.rest_4_ = bf16[96,768]{1,0:T(8,128)(2,1)S(1)} collective-permute-done((bf16[96,768]{1,0:T(8,128)(2,1)S(1)}, bf16[96,768]{1,0:T(8,128)(2,1)S(1)}, u32[]{:S(2)}, u32[]{:S(2)}) %collective-permute-start.6) | collective-permute-done | bytes 147488 | tf_op jit(solution)/shard_map/ppermute | solution.py:575
  55.8 6.7 %collective-permute-done.9.rest_7_ = bf16[96,768]{1,0:T(8,128)(2,1)S(1)} collective-permute-done((bf16[96,768]{1,0:T(8,128)(2,1)S(1)}, bf16[96,768]{1,0:T(8,128)(2,1)S(1)}, u32[]{:S(2)}, u32[]{:S(2)}) %collective-permute-start.9) | collective-permute-done | bytes 147488 | tf_op jit(solution)/shard_map/ppermute | solution.py:575
  64.3 9.4 %qkv.1 = (bf16[2048,768]{1,0:T(8,128)(2,1)}, bf16[576,2048]{1,0:T(8,128)(2,1)}, bf16[2048,192]{1,0:T(8,128)(2,1)}, bf16[2048,192]{1,0:T(8,128)(2,1)}, bf16[768,768]{1,0:T(8,128)(2,1)}) custom-call(s32[24]{0:T(128)} %concatenate.27.sc, bf16[512,768]{1,0:T(8,128)(2,1)} %tokens.3, bf16[512,768]{1,0:T(8,128)(2,1)} %copy-done.7, bf16[512,768]{1,0:T(8,128)(2,1)} %copy-done.8, ...), custom_call_target="tpu_custom_call" | custom-call | tf_op jit(solution)/shard_map/qkv/pallas_call | solution.py:76
  75.0 8.4 %attention.2 = (bf16[192,1024]{1,0:T(8,128)(2,1)}, f32[8,1024]{1,0:T(8,128)}) custom-call(s32[24]{0:T(128)} %concatenate.27.sc, bf16[576,2048]{1,0:T(8,128)(2,1)} %get-tuple-element.67.qt.vt.kt, bf16[2048,192]{1,0:T(8,128)(2,1)} %get-tuple-element.68.kn, bf16[576,2048]{1,0:T(8,128)(2,1)} %get-tuple-element.67.qt.vt.kt, s32[1,2048]{1,0:T(1,128)} %get-tuple-element.135.gq, ...), custom_call_target="tpu_custom_call" | custom-call | tf_op jit(solution)/shard_map/attention/pallas_call | solution.py:188
  83.4 4.8 %collective-permute-start.10 = (bf16[192,1024]{1,0:T(8,128)(2,1)}, bf16[192,1024]{1,0:T(8,128)(2,1)S(1)}, u32[]{:S(2)}, u32[]{:S(2)}) collective-permute-start(bf16[192,1024]{1,0:T(8,128)(2,1)} %get-tuple-element.69.ot), channel_id=1, source_target_pairs={{0,2},{1,3},{2,0},{3,1},{4,6},{5,7},{6,4},{7,5},{8,10},{9,11},{10,... | collective-permute-start | bytes 1179656 | tf_op jit(solution)/shard_map/ppermute | solution.py:572
  89.3 11.9 %attention.3 = (bf16[192,1024]{1,0:T(8,128)(2,1)}, f32[8,1024]{1,0:T(8,128)}) custom-call(s32[24]{0:T(128)} %concatenate.27.sc, bf16[576,2048]{1,0:T(8,128)(2,1)} %get-tuple-element.67.qt.vt.kt, bf16[2048,192]{1,0:T(8,128)(2,1)} %get-tuple-element.68.kn, bf16[576,2048]{1,0:T(8,128)(2,1)} %get-tuple-element.67.qt.vt.kt, s32[1,2048]{1,0:T(1,128)} %get-tuple-element.135.gq, ...), custom_call_target="tpu_custom_call" | custom-call | tf_op jit(solution)/shard_map/attention/pallas_call | solution.py:188
  103.5 3.6 out_projection.1
  110.5 4.1 %middle.1 = (f32[512,768]{1,0:T(8,128)}, bf16[512,768]{1,0:T(8,128)(2,1)}) custom-call(bf16[512,768]{1,0:T(8,128)(2,1)} %tokens.3, f32[512,768]{1,0:T(8,128)} %get-tuple-element.73.own, bf16[512,768]{1,0:T(8,128)(2,1)} %copy-done.23, f32[1,768]{1,0:T(1,128)} %broadcast_in_dim.37.gain), custom_call_target="tpu_custom_call" | custom-call | tf_op jit(solution)/shard_map/middle/pallas_call | solution.py:338
  116.3 11.7 %collective-permute-done.18.ya = bf16[512,768]{1,0:T(8,128)(2,1)S(1)} collective-permute-done((bf16[512,768]{1,0:T(8,128)(2,1)S(1)}, bf16[512,768]{1,0:T(8,128)(2,1)S(1)}, u32[]{:S(2)}, u32[]{:S(2)}) %collective-permute-start.18) | collective-permute-done | bytes 786464 | tf_op jit(solution)/shard_map/ppermute | solution.py:572
  128.0 16.5 %collective-permute-done.16.na = bf16[512,768]{1,0:T(8,128)(2,1)S(1)} collective-permute-done((bf16[512,768]{1,0:T(8,128)(2,1)}, bf16[512,768]{1,0:T(8,128)(2,1)S(1)}, u32[]{:S(2)}, u32[]{:S(2)}) %collective-permute-start.16) | collective-permute-done | bytes 786464 | tf_op jit(solution)/shard_map/ppermute | solution.py:572
  146.9 10.4 %mlp.3 = (bf16[512,768]{1,0:T(8,128)(2,1)}, bf16[512,768]{1,0:T(8,128)(2,1)}, bf16[512,768]{1,0:T(8,128)(2,1)}, bf16[512,768]{1,0:T(8,128)(2,1)}, bf16[1024,512]{1,0:T(8,128)(2,1)}, /*index=5*/bf16[1024,1024]{1,0:T(8,128)(2,1)}) custom-call(bf16[512,768]{1,0:T(8,128)(2,1)} %copy-done.14, bf16[512,768]{1,0:T(8,128)(2,1)} %collective-permute-done.17.nb, ...), custom_call_target="tpu_custom_call" | custom-call | tf_op jit(solution)/shard_map/mlp/pallas_call | solution.py:390
  157.5 10.4 %mlp.2 = (bf16[512,768]{1,0:T(8,128)(2,1)}, bf16[512,768]{1,0:T(8,128)(2,1)}, bf16[512,768]{1,0:T(8,128)(2,1)}, bf16[512,768]{1,0:T(8,128)(2,1)}, bf16[1024,512]{1,0:T(8,128)(2,1)}, /*index=5*/bf16[1024,1024]{1,0:T(8,128)(2,1)}) custom-call(bf16[512,768]{1,0:T(8,128)(2,1)} %get-tuple-element.76.na, bf16[512,768]{1,0:T(8,128)(2,1)} %collective-permute-done.13.nb, ...), custom_call_target="tpu_custom_call" | custom-call | tf_op jit(solution)/shard_map/mlp/pallas_call | solution.py:390
  170.4 5.3 %fusion = f32[768,1024]{1,0:T(8,128)} fusion(bf16[1024,1024]{1,0:T(8,128)(2,1)} %get-tuple-element.115, bf16[512,768]{1,0:T(8,128)(2,1)} %collective-permute-done.13.nb, bf16[512,768]{1,0:T(8,128)(2,1)S(1)} %copy-done.16), kind=kOutput, calls=%fused_computation.6 | convolution fusion | flops 1613758464 | bytes 6815744 | tf_op jit(solution)/shard_map/dot_general | solution.py:28
  175.8 12.5 %collective-permute-done.21.c = bf16[512,768]{1,0:T(8,128)(2,1)S(1)} collective-permute-done((bf16[512,768]{1,0:T(8,128)(2,1)S(1)}, bf16[512,768]{1,0:T(8,128)(2,1)S(1)}, u32[]{:S(2)}, u32[]{:S(2)}) %collective-permute-start.21) | collective-permute-done | bytes 786464 | tf_op jit(solution)/shard_map/ppermute | solution.py:572
  189.1 4.9 %middle_back.1 = (f32[512,768]{1,0:T(8,128)}, bf16[512,768]{1,0:T(8,128)(2,1)}, f32[1,768]{1,0:T(1,128)}) custom-call(bf16[512,768]{1,0:T(8,128)(2,1)} %dy.1, f32[512,768]{1,0:T(8,128)} %get-tuple-element.75.h1_r, bf16[512,768]{1,0:T(8,128)(2,1)} %get-tuple-element.86.a, bf16[512,768]{1,0:T(8,128)(2,1)} %copy-done.17, bf16[512,768]{1,0:T(8,128)(2,1)} %copy-done.18, ...), custom_call_target="tpu_custom_call" | custom-call | tf_op jit(solution)/shard_map/middle_back/pallas_call | solution.py:431
  194.1 3.4 fusion.7
  200.7 4.4 %out_back.1 = (bf16[192,1024]{1,0:T(8,128)(2,1)}, bf16[192,1024]{1,0:T(8,128)(2,1)}, f32[192,768]{1,0:T(8,128)}, bf16[192,768]{1,0:T(8,128)(2,1)}) custom-call(bf16[512,768]{1,0:T(8,128)(2,1)} %get-tuple-element.90.own, bf16[512,768]{1,0:T(8,128)(2,1)} %collective-permute-done.25.other, bf16[192,768]{1,0:T(8,128)(2,1)} %copy-done.3, ...), custom_call_target="tpu_custom_call" | custom-call | tf_op jit(solution)/shard_map/out_back/pallas_call | solution.py:453
  206.8 3.7 add_convert_fusion.1
  210.5 4.2 %collective-permute-done.37 = bf16[192,768]{1,0:T(8,128)(2,1)S(1)} collective-permute-done((bf16[192,768]{1,0:T(8,128)(2,1)}, bf16[192,768]{1,0:T(8,128)(2,1)S(1)}, u32[]{:S(2)}, u32[]{:S(2)}) %collective-permute-start.37) | collective-permute-done | bytes 294944 | tf_op jit(solution)/shard_map/ppermute | solution.py:572
  219.4 19.5 %attention_back.2 = (bf16[192,1024]{1,0:T(8,128)(2,1)}, f32[192,2048]{1,0:T(8,128)}, f32[192,2048]{1,0:T(8,128)}) custom-call(s32[24]{0:T(128)} %concatenate.27.sc, bf16[576,2048]{1,0:T(8,128)(2,1)} %get-tuple-element.67.qt.vt.kt, bf16[2048,192]{1,0:T(8,128)(2,1)} %get-tuple-element.68.kn, bf16[576,2048]{1,0:T(8,128)(2,1)} %get-tuple-element.67.qt.vt.kt, ...), custom_call_target="tpu_custom_call" | custom-call | tf_op jit(solution)/shard_map/attention_back/pallas_call | solution.py:275
  239.7 14.6 %attention_back.3 = (bf16[192,1024]{1,0:T(8,128)(2,1)}, bf16[192,2048]{1,0:T(8,128)(2,1)}, bf16[192,2048]{1,0:T(8,128)(2,1)}) custom-call(s32[24]{0:T(128)} %concatenate.27.sc, bf16[576,2048]{1,0:T(8,128)(2,1)} %get-tuple-element.67.qt.vt.kt, bf16[2048,192]{1,0:T(8,128)(2,1)} %get-tuple-element.68.kn, bf16[576,2048]{1,0:T(8,128)(2,1)} %get-tuple-element.67.qt.vt.kt, ...), custom_call_target="tpu_custom_call" | custom-call | tf_op jit(solution)/shard_map/attention_back/pallas_call | solution.py:275
  254.3 4.2 %rows_back.3 = (bf16[512,768]{1,0:T(8,128)(2,1)}, bf16[512,768]{1,0:T(8,128)(2,1)}) custom-call(bf16[192,2048]{1,0:T(8,128)(2,1)} %get-tuple-element.105.dk, bf16[192,1024]{1,0:T(8,128)(2,1)} %get-tuple-element.102.dq.dqb, bf16[192,2048]{1,0:T(8,128)(2,1)} %get-tuple-element.99.dv, bf16[768,768]{1,0:T(8,128)(2,1)} %get-tuple-element.72.wt), custom_call_target="tpu_custom_call" | custom-call | tf_op jit(solution)/shard_map/rows_back/pallas_call | solution.py:477
  258.5 6.1 %weights_back.1 = (f32[1,768]{1,0:T(1,128)}, bf16[96,576]{1,0:T(8,128)(2,1)}, bf16[96,576]{1,0:T(8,128)(2,1)}, bf16[96,576]{1,0:T(8,128)(2,1)}, bf16[96,576]{1,0...) custom-call(s32[24]{0:T(128)} %concatenate.27.sc, ...), custom_call_target="tpu_custom_call" | custom-call | tf_op jit(solution)/shard_map/weights_back/pallas_call | solution.py:512
  267.7 3.5 collective-permute-done.39
  271.9 3.6 collective-permute-done.40
  275.6 30.6 %collective-permute-start.41 = (f32[2,768]{1,0:T(2,128)S(1)}, f32[2,768]{1,0:T(2,128)S(1)}, u32[]{:S(2)}, u32[]{:S(2)}) collective-permute-start(f32[2,768]{1,0:T(2,128)S(1)} %add.117), channel_id=1, source_target_pairs={{0,8},{4,12},{8,0},{12,4},{16,24},{20,28},{24,16},{28,20},{1,9},{5... | collective-permute-start | bytes 18440 | tf_op jit(solution)/shard_map/ppermute | solution.py:575
  312.4 4.2 %rows_back.2 = (bf16[512,768]{1,0:T(8,128)(2,1)}, bf16[512,768]{1,0:T(8,128)(2,1)}) custom-call(bf16[192,2048]{1,0:T(8,128)(2,1)} %get-tuple-element.105.dk, bf16[192,1024]{1,0:T(8,128)(2,1)} %get-tuple-element.98.dq.dqa, bf16[192,2048]{1,0:T(8,128)(2,1)} %get-tuple-element.99.dv, bf16[768,768]{1,0:T(8,128)(2,1)} %get-tuple-element.72.wt), custom_call_target="tpu_custom_call" | custom-call | tf_op jit(solution)/shard_map/rows_back/pallas_call | solution.py:477
  324.8 5.7 %collective-permute-done.34 = bf16[96,576]{1,0:T(8,128)(2,1)S(1)} collective-permute-done((bf16[96,576]{1,0:T(8,128)(2,1)}, bf16[96,576]{1,0:T(8,128)(2,1)S(1)}, u32[]{:S(2)}, u32[]{:S(2)}) %collective-permute-start.34) | collective-permute-done | bytes 110624 | tf_op jit(solution)/shard_map/ppermute | solution.py:575
  342.5 15.0 %collective-permute-done.29.c = bf16[512,768]{1,0:T(8,128)(2,1)S(1)} collective-permute-done((bf16[512,768]{1,0:T(8,128)(2,1)S(1)}, bf16[512,768]{1,0:T(8,128)(2,1)S(1)}, u32[]{:S(2)}, u32[]{:S(2)}) %collective-permute-start.29) | collective-permute-done | bytes 786464 | tf_op jit(solution)/shard_map/ppermute | solution.py:572
  358.4 4.5 %last.1 = bf16[512,768]{1,0:T(8,128)(2,1)} custom-call(bf16[512,768]{1,0:T(8,128)(2,1)} %tokens.3, f32[512,768]{1,0:T(8,128)} %get-tuple-element.88.dh1, bf16[512,768]{1,0:T(8,128)(2,1)} %get-tuple-element.100.a, bf16[512,768]{1,0:T(8,128)(2,1)} %copy-done.24, bf16[512,768]{1,0:T(8,128)(2,1)} %copy-done.25, f32[1,768]{1,0:T(1,128)} %broadcast_in_dim.29.gain), custom_call_target="tpu_custom_call" | custom-call | tf_op jit(solution)/shard_map/last/pallas_call | solution.py:537
  (224 shorter events, 89.9 us)
Async XLA Ops:
  7.2 137.8 %all-gather.2.cloned.1.call-start = ((), (), s32[]{:S(2)}) async-start(), calls=%async_computation.1 | async-start | bytes 2654208 | tf_op jit(solution)/shard_map/all_gather | solution.py:590
  7.2 55.2 %collective-permute-start = (bf16[512,768]{1,0:T(8,128)(2,1)}, bf16[512,768]{1,0:T(8,128)(2,1)S(1)}, u32[]{:S(2)}, u32[]{:S(2)}) collective-permute-start(bf16[512,768]{1,0:T(8,128)(2,1)} %tokens.3), channel_id=1, source_target_pairs={{0,1},{1,0},{2,3},{3,2},{4,5},{5,4},{6,7},{7,6},{8,9},{9,8},{10,11... | collective-permute-start | bytes 2359304 | tf_op jit(solution)/shard_map/ppermute | solution.py:569
  7.8 20.9 %collective-permute-start.1 = (bf16[512,768]{1,0:T(8,128)(2,1)}, bf16[512,768]{1,0:T(8,128)(2,1)S(1)}, u32[]{:S(2)}, u32[]{:S(2)}) collective-permute-start(bf16[512,768]{1,0:T(8,128)(2,1)} %tokens.3), channel_id=1, source_target_pairs={{0,2},{1,3},{2,0},{3,1},{4,6},{5,7},{6,4},{7,5},{8,10},{9,11},{10,... | collective-permute-start | bytes 2359304 | tf_op jit(solution)/shard_map/ppermute | solution.py:572
  11.3 20.8 %collective-permute-start.3 = (bf16[96,768]{1,0:T(8,128)(2,1)S(1)}, bf16[96,768]{1,0:T(8,128)(2,1)S(1)}, u32[]{:S(2)}, u32[]{:S(2)}) collective-permute-start(bf16[96,768]{1,0:T(8,128)(2,1)S(1)} %pad_maximum_fusion.2.rest_0_), channel_id=1, source_target_pairs={{0,4},{4,0},{8,12},{12,8},{16,20},{20,16},{24,28},{28,24},{1,5},{5... | collective-permute-start | bytes 442376 | tf_op jit(solution)/shard_map/ppermute | solution.py:575
  12.9 22.8 %collective-permute-start.4 = (bf16[96,768]{1,0:T(8,128)(2,1)S(1)}, bf16[96,768]{1,0:T(8,128)(2,1)S(1)}, u32[]{:S(2)}, u32[]{:S(2)}) collective-permute-start(bf16[96,768]{1,0:T(8,128)(2,1)S(1)} %pad_maximum_fusion.2.rest_0_), channel_id=1, source_target_pairs={{0,8},{4,12},{8,0},{12,4},{16,24},{20,28},{24,16},{28,20},{1,9},{5... | collective-permute-start | bytes 442376 | tf_op jit(solution)/shard_map/ppermute | solution.py:575
  14.5 22.5 %collective-permute-start.5 = (bf16[96,768]{1,0:T(8,128)(2,1)S(1)}, bf16[96,768]{1,0:T(8,128)(2,1)S(1)}, u32[]{:S(2)}, u32[]{:S(2)}) collective-permute-start(bf16[96,768]{1,0:T(8,128)(2,1)S(1)} %pad_maximum_fusion.2.rest_0_), channel_id=1, source_target_pairs={{0,12},{4,8},{8,4},{12,0},{16,28},{20,24},{24,20},{28,16},{1,13},{... | collective-permute-start | bytes 442376 | tf_op jit(solution)/shard_map/ppermute | solution.py:575
  16.6 346.2 %reduce-scatter.2.cloned.1.call-start = ((), (), s32[]{:S(2)}) async-start(), calls=%async_computation.2 | async-start | bytes 3096576 | tf_op jit(solution)/shard_map/reduce_scatter | solution.py:653
  28.7 33.8 %collective-permute-start.2 = (bf16[512,768]{1,0:T(8,128)(2,1)S(1)}, bf16[512,768]{1,0:T(8,128)(2,1)S(1)}, u32[]{:S(2)}, u32[]{:S(2)}) collective-permute-start(bf16[512,768]{1,0:T(8,128)(2,1)S(1)} %collective-permute-done.1.t2), channel_id=1, source_target_pairs={{0,1},{1,0},{2,3},{3,2},{4,5},{5,4},{6,7},{7,6},{8,9},{9,8},{10,11... | collective-permute-start | bytes 2359304 | tf_op jit(solution)/shard_map/ppermute | solution.py:569
  32.1 19.9 %collective-permute-start.6 = (bf16[96,768]{1,0:T(8,128)(2,1)S(1)}, bf16[96,768]{1,0:T(8,128)(2,1)S(1)}, u32[]{:S(2)}, u32[]{:S(2)}) collective-permute-start(bf16[96,768]{1,0:T(8,128)(2,1)S(1)} %pad_maximum_fusion.2.rest_0_), channel_id=1, source_target_pairs={{0,16},{4,20},{8,24},{12,28},{16,0},{20,4},{24,8},{28,12},{1,17},{... | collective-permute-start | bytes 442376 | tf_op jit(solution)/shard_map/ppermute | solution.py:575
  35.7 20.1 %collective-permute-start.7 = (bf16[96,768]{1,0:T(8,128)(2,1)S(1)}, bf16[96,768]{1,0:T(8,128)(2,1)S(1)}, u32[]{:S(2)}, u32[]{:S(2)}) collective-permute-start(bf16[96,768]{1,0:T(8,128)(2,1)S(1)} %pad_maximum_fusion.2.rest_0_), channel_id=1, source_target_pairs={{0,20},{4,16},{8,28},{12,24},{16,4},{20,0},{24,12},{28,8},{1,21},{... | collective-permute-start | bytes 442376 | tf_op jit(solution)/shard_map/ppermute | solution.py:575
  37.0 18.8 %collective-permute-start.8 = (bf16[96,768]{1,0:T(8,128)(2,1)S(1)}, bf16[96,768]{1,0:T(8,128)(2,1)S(1)}, u32[]{:S(2)}, u32[]{:S(2)}) collective-permute-start(bf16[96,768]{1,0:T(8,128)(2,1)S(1)} %pad_maximum_fusion.2.rest_0_), channel_id=1, source_target_pairs={{0,24},{4,28},{8,16},{12,20},{16,8},{20,12},{24,0},{28,4},{1,25},{... | collective-permute-start | bytes 442376 | tf_op jit(solution)/shard_map/ppermute | solution.py:575
  52.0 10.5 %collective-permute-start.9 = (bf16[96,768]{1,0:T(8,128)(2,1)S(1)}, bf16[96,768]{1,0:T(8,128)(2,1)S(1)}, u32[]{:S(2)}, u32[]{:S(2)}) collective-permute-start(bf16[96,768]{1,0:T(8,128)(2,1)S(1)} %pad_maximum_fusion.2.rest_0_), channel_id=1, source_target_pairs={{0,28},{4,24},{8,20},{12,16},{16,12},{20,8},{24,4},{28,0},{1,29},{... | collective-permute-start | bytes 442376 | tf_op jit(solution)/shard_map/ppermute | solution.py:575
  83.4 19.3 %collective-permute-start.10 = (bf16[192,1024]{1,0:T(8,128)(2,1)}, bf16[192,1024]{1,0:T(8,128)(2,1)S(1)}, u32[]{:S(2)}, u32[]{:S(2)}) collective-permute-start(bf16[192,1024]{1,0:T(8,128)(2,1)} %get-tuple-element.69.ot), channel_id=1, source_target_pairs={{0,2},{1,3},{2,0},{3,1},{4,6},{5,7},{6,4},{7,5},{8,10},{9,11},{10,... | collective-permute-start | bytes 1179656 | tf_op jit(solution)/shard_map/ppermute | solution.py:572
  89.2 13.4 %collective-permute-start.11 = (bf16[192,768]{1,0:T(8,128)(2,1)S(1)}, bf16[192,768]{1,0:T(8,128)(2,1)S(1)}, u32[]{:S(2)}, u32[]{:S(2)}) collective-permute-start(bf16[192,768]{1,0:T(8,128)(2,1)S(1)} %slice.38.wm), channel_id=1, source_target_pairs={{0,2},{1,3},{2,0},{3,1},{4,6},{5,7},{6,4},{7,5},{8,10},{9,11},{10,... | collective-permute-start | bytes 884744 | tf_op jit(solution)/shard_map/ppermute | solution.py:572
  107.7 20.3 %collective-permute-start.18 = (bf16[512,768]{1,0:T(8,128)(2,1)S(1)}, bf16[512,768]{1,0:T(8,128)(2,1)S(1)}, u32[]{:S(2)}, u32[]{:S(2)}) collective-permute-start(bf16[512,768]{1,0:T(8,128)(2,1)S(1)} %copy-done.1), channel_id=1, source_target_pairs={{0,2},{1,3},{2,0},{3,1},{4,6},{5,7},{6,4},{7,5},{8,10},{9,11},{10,... | collective-permute-start | bytes 2359304 | tf_op jit(solution)/shard_map/ppermute | solution.py:572
  114.5 29.9 %collective-permute-start.16 = (bf16[512,768]{1,0:T(8,128)(2,1)}, bf16[512,768]{1,0:T(8,128)(2,1)S(1)}, u32[]{:S(2)}, u32[]{:S(2)}) collective-permute-start(bf16[512,768]{1,0:T(8,128)(2,1)} %get-tuple-element.76.na), channel_id=1, source_target_pairs={{0,2},{1,3},{2,0},{3,1},{4,6},{5,7},{6,4},{7,5},{8,10},{9,11},{10,... | collective-permute-start | bytes 2359304 | tf_op jit(solution)/shard_map/ppermute | solution.py:572
  128.0 17.0 %collective-permute-start.19 = (bf16[512,768]{1,0:T(8,128)(2,1)S(1)}, bf16[512,768]{1,0:T(8,128)(2,1)S(1)}, u32[]{:S(2)}, u32[]{:S(2)}) collective-permute-start(bf16[512,768]{1,0:T(8,128)(2,1)S(1)} %collective-permute-done.18.ya), channel_id=1, source_target_pairs={{0,1},{1,0},{2,3},{3,2},{4,5},{5,4},{6,7},{7,6},{8,9},{9,8},{10,11... | collective-permute-start | bytes 2359304 | tf_op jit(solution)/shard_map/ppermute | solution.py:569
  144.5 13.0 %collective-permute-start.14 = (bf16[512,768]{1,0:T(8,128)(2,1)S(1)}, bf16[512,768]{1,0:T(8,128)(2,1)}, u32[]{:S(2)}, u32[]{:S(2)}) collective-permute-start(bf16[512,768]{1,0:T(8,128)(2,1)S(1)} %copy-done.1), channel_id=1, source_target_pairs={{0,1},{1,0},{2,3},{3,2},{4,5},{5,4},{6,7},{7,6},{8,9},{9,8},{10,11... | collective-permute-start | bytes 2359304 | tf_op jit(solution)/shard_map/ppermute | solution.py:569
  145.0 12.5 %collective-permute-start.13 = (bf16[512,768]{1,0:T(8,128)(2,1)}, bf16[512,768]{1,0:T(8,128)(2,1)}, u32[]{:S(2)}, u32[]{:S(2)}) collective-permute-start(bf16[512,768]{1,0:T(8,128)(2,1)} %get-tuple-element.76.na), channel_id=1, source_target_pairs={{0,1},{1,0},{2,3},{3,2},{4,5},{5,4},{6,7},{7,6},{8,9},{9,8},{10,11... | collective-permute-start | bytes 2359304 | tf_op jit(solution)/shard_map/ppermute | solution.py:569
  157.3 11.1 %collective-permute-start.20 = (bf16[512,768]{1,0:T(8,128)(2,1)}, bf16[512,768]{1,0:T(8,128)(2,1)S(1)}, u32[]{:S(2)}, u32[]{:S(2)}) collective-permute-start(bf16[512,768]{1,0:T(8,128)(2,1)} %get-tuple-element.82), channel_id=1, source_target_pairs={{0,1},{1,0},{2,3},{3,2},{4,5},{5,4},{6,7},{7,6},{8,9},{9,8},{10,11... | collective-permute-start | bytes 2359304 | tf_op jit(solution)/shard_map/ppermute | solution.py:569
  168.6 19.7 %collective-permute-start.21 = (bf16[512,768]{1,0:T(8,128)(2,1)S(1)}, bf16[512,768]{1,0:T(8,128)(2,1)S(1)}, u32[]{:S(2)}, u32[]{:S(2)}) collective-permute-start(bf16[512,768]{1,0:T(8,128)(2,1)S(1)} %add_convert_fusion.5), channel_id=1, source_target_pairs={{0,2},{1,3},{2,0},{3,1},{4,6},{5,7},{6,4},{7,5},{8,10},{9,11},{10,... | collective-permute-start | bytes 2359304 | tf_op jit(solution)/shard_map/ppermute | solution.py:572
  217.7 21.2 %collective-permute-start.26 = (bf16[192,1024]{1,0:T(8,128)(2,1)S(1)}, bf16[192,1024]{1,0:T(8,128)(2,1)S(1)}, u32[]{:S(2)}, u32[]{:S(2)}) collective-permute-start(bf16[192,1024]{1,0:T(8,128)(2,1)S(1)} %copy-done.45), channel_id=1, source_target_pairs={{0,2},{1,3},{2,0},{3,1},{4,6},{5,7},{6,4},{7,5},{8,10},{9,11},{10,... | collective-permute-start | bytes 1179656 | tf_op jit(solution)/shard_map/ppermute | solution.py:572
  219.4 90.0 %collective-permute-start.22 = (bf16[512,768]{1,0:T(8,128)(2,1)}, bf16[512,768]{1,0:T(8,128)(2,1)S(1)}, u32[]{:S(2)}, u32[]{:S(2)}) collective-permute-start(bf16[512,768]{1,0:T(8,128)(2,1)} %get-tuple-element.85), channel_id=1, source_target_pairs={{0,1},{1,0},{2,3},{3,2},{4,5},{5,4},{6,7},{7,6},{8,9},{9,8},{10,11... | collective-permute-start | bytes 2359304 | tf_op jit(solution)/shard_map/ppermute | solution.py:569
  265.9 66.9 %collective-permute-start.28 = (bf16[512,768]{1,0:T(8,128)(2,1)}, bf16[512,768]{1,0:T(8,128)(2,1)S(1)}, u32[]{:S(2)}, u32[]{:S(2)}) collective-permute-start(bf16[512,768]{1,0:T(8,128)(2,1)} %get-tuple-element.104), channel_id=1, source_target_pairs={{0,1},{1,0},{2,3},{3,2},{4,5},{5,4},{6,7},{7,6},{8,9},{9,8},{10,11... | collective-permute-start | bytes 2359304 | tf_op jit(solution)/shard_map/ppermute | solution.py:569
  275.6 32.2 %collective-permute-start.41 = (f32[2,768]{1,0:T(2,128)S(1)}, f32[2,768]{1,0:T(2,128)S(1)}, u32[]{:S(2)}, u32[]{:S(2)}) collective-permute-start(f32[2,768]{1,0:T(2,128)S(1)} %add.117), channel_id=1, source_target_pairs={{0,8},{4,12},{8,0},{12,4},{16,24},{20,28},{24,16},{28,20},{1,9},{5... | collective-permute-start | bytes 18440 | tf_op jit(solution)/shard_map/ppermute | solution.py:575
  306.1 35.1 %collective-permute-start.15 = (bf16[512,768]{1,0:T(8,128)(2,1)}, bf16[512,768]{1,0:T(8,128)(2,1)S(1)}, u32[]{:S(2)}, u32[]{:S(2)}) collective-permute-start(bf16[512,768]{1,0:T(8,128)(2,1)} %get-tuple-element.79), channel_id=1, source_target_pairs={{0,1},{1,0},{2,3},{3,2},{4,5},{5,4},{6,7},{7,6},{8,9},{9,8},{10,11... | collective-permute-start | bytes 2359304 | tf_op jit(solution)/shard_map/ppermute | solution.py:569
  306.1 13.6 %collective-permute-start.36 = (bf16[96,576]{1,0:T(8,128)(2,1)}, bf16[96,576]{1,0:T(8,128)(2,1)S(1)}, u32[]{:S(2)}, u32[]{:S(2)}) collective-permute-start(bf16[96,576]{1,0:T(8,128)(2,1)} %get-tuple-element.114), channel_id=1, source_target_pairs={{0,28},{4,24},{8,20},{12,16},{16,12},{20,8},{24,4},{28,0},{1,29},{... | collective-permute-start | bytes 331784 | tf_op jit(solution)/shard_map/ppermute | solution.py:575
  307.7 13.1 %collective-permute-start.35 = (bf16[96,576]{1,0:T(8,128)(2,1)}, bf16[96,576]{1,0:T(8,128)(2,1)S(1)}, u32[]{:S(2)}, u32[]{:S(2)}) collective-permute-start(bf16[96,576]{1,0:T(8,128)(2,1)} %get-tuple-element.113), channel_id=1, source_target_pairs={{0,24},{4,28},{8,16},{12,20},{16,8},{20,12},{24,0},{28,4},{1,25},{... | collective-permute-start | bytes 331784 | tf_op jit(solution)/shard_map/ppermute | solution.py:575
  319.2 22.0 %collective-permute-start.23 = (bf16[512,768]{1,0:T(8,128)(2,1)S(1)}, bf16[512,768]{1,0:T(8,128)(2,1)S(1)}, u32[]{:S(2)}, u32[]{:S(2)}) collective-permute-start(bf16[512,768]{1,0:T(8,128)(2,1)S(1)} %copy-done.21), channel_id=1, source_target_pairs={{0,2},{1,3},{2,0},{3,1},{4,6},{5,7},{6,4},{7,5},{8,10},{9,11},{10,... | collective-permute-start | bytes 2359304 | tf_op jit(solution)/shard_map/ppermute | solution.py:572
  319.7 10.8 %collective-permute-start.34 = (bf16[96,576]{1,0:T(8,128)(2,1)}, bf16[96,576]{1,0:T(8,128)(2,1)S(1)}, u32[]{:S(2)}, u32[]{:S(2)}) collective-permute-start(bf16[96,576]{1,0:T(8,128)(2,1)} %get-tuple-element.112), channel_id=1, source_target_pairs={{0,20},{4,16},{8,28},{12,24},{16,4},{20,0},{24,12},{28,8},{1,21},{... | collective-permute-start | bytes 331784 | tf_op jit(solution)/shard_map/ppermute | solution.py:575
  320.8 11.7 %collective-permute-start.33 = (bf16[96,576]{1,0:T(8,128)(2,1)}, bf16[96,576]{1,0:T(8,128)(2,1)S(1)}, u32[]{:S(2)}, u32[]{:S(2)}) collective-permute-start(bf16[96,576]{1,0:T(8,128)(2,1)} %get-tuple-element.111), channel_id=1, source_target_pairs={{0,16},{4,20},{8,24},{12,28},{16,0},{20,4},{24,8},{28,12},{1,17},{... | collective-permute-start | bytes 331784 | tf_op jit(solution)/shard_map/ppermute | solution.py:575
  338.8 18.7 %collective-permute-start.29 = (bf16[512,768]{1,0:T(8,128)(2,1)S(1)}, bf16[512,768]{1,0:T(8,128)(2,1)S(1)}, u32[]{:S(2)}, u32[]{:S(2)}) collective-permute-start(bf16[512,768]{1,0:T(8,128)(2,1)S(1)} %add_convert_fusion.2), channel_id=1, source_target_pairs={{0,2},{1,3},{2,0},{3,1},{4,6},{5,7},{6,4},{7,5},{8,10},{9,11},{10,... | collective-permute-start | bytes 2359304 | tf_op jit(solution)/shard_map/ppermute | solution.py:572
  (61 other events, 646.9 us)
Sparse Core Ops, SparseCore 0:
  16.7 67.3 all-gather.1
  216.8 87.2 reduce-scatter.1

commit v2 on v1

--- a/solution.py
+++ b/solution.py
@@ -10,6 +10,8 @@
 HEAD = 64
 BLK = 256
 DIRECT = 8
+FOLD = 32
+EXTRA = 8
 eps_norm = 1e-06
 neg_large = -1e30
 F32 = jnp.float32
@@ -96,6 +98,7 @@
         ],
         scratch_shapes=[pltpu.VMEM((rows, width), BF16), pltpu.VMEM((width, 4 * cols), BF16)],
         name="qkv",
+        cost_estimate=cost(0.01),
     )(sc, *shards, gain, *pieces)
 
 
@@ -108,6 +111,10 @@
 
 def placed(block, me, per):
     return ((block // per) ^ me) * per + lax.rem(block, per)
+
+
+def cost(us):
+    return pl.CostEstimate(flops=int(us * 1e9), transcendentals=0, bytes_accessed=1024)
 
 
 def span(sc, half, per, blocks):
@@ -121,14 +128,14 @@
     def at(t):
         block = low + t
         block = block + (block >= place).astype(jnp.int32)
-        return placed(block, me, per)
-
-    return stored, count, at
-
-
-def allowed(gkv, gq, start, own):
-    keys = gkv[pl.ds(start, BLK), :]
-    mask = jnp.concatenate([keys] * (BLK // 128), axis=1) == gq[...]
+        return block, pl.multiple_of(placed(block, me, per) * BLK, BLK)
+
+    return stored, place, count, at
+
+
+def allowed(gkv, queries, block, own):
+    keys = gkv[pl.ds(pl.multiple_of(block * BLK, BLK), BLK), :]
+    mask = jnp.concatenate([keys] * (BLK // 128), axis=1) == queries
     if own:
         mask = mask | (
             lax.broadcasted_iota(jnp.int32, (BLK, BLK), 0)
@@ -139,11 +146,12 @@
 
 def forward_kernel(half, per, sc, qt, kn, vt, gq, gkv, ot, lse, zq):
     heads = qt.shape[0] // HEAD
-    stored, count, at = span(sc, half, per, pl.num_programs(0))
+    stored, place, count, at = span(sc, half, per, pl.num_programs(0))
     spread(qt, zq)
-
-    def scores(start, own):
-        mask = allowed(gkv, gq, start, own)
+    queries = gq[:, pl.ds(pl.multiple_of(place * BLK, BLK), BLK)]
+
+    def scores(block, start, own):
+        mask = allowed(gkv, queries, block, own)
         keys = kn[pl.ds(start, BLK), :]
         return [jnp.where(mask, nn(keys, zq[h]), neg_large) for h in range(heads)]
 
@@ -152,15 +160,15 @@
 
     start = pl.multiple_of(stored * BLK, BLK)
     carry = []
-    for h, s in enumerate(scores(start, True)):
+    for h, s in enumerate(scores(place, start, True)):
         top = jnp.max(s, axis=0, keepdims=True)
         p = jnp.exp(s - top)
         carry.append((top, jnp.sum(p, axis=0, keepdims=True), mixed(h, start, p)))
 
     def body(t, carry):
-        start = pl.multiple_of(at(t) * BLK, BLK)
+        block, start = at(t)
         out = []
-        for h, s in enumerate(scores(start, False)):
+        for h, s in enumerate(scores(block, start, False)):
             top, total, acc = carry[h]
             higher = jnp.maximum(top, jnp.max(s, axis=0, keepdims=True))
             p = jnp.exp(s - higher)
@@ -193,7 +201,7 @@
             pl.BlockSpec((cols, BLK), lambda i: (1, half * blocks + i)),
             whole((total, cols)),
             pl.BlockSpec((cols, total), lambda i: (2, 0)),
-            pl.BlockSpec((1, BLK), lambda i: (0, half * blocks + i)),
+            whole((1, total)),
             whole((total, 128)),
         ],
         out_specs=[
@@ -203,29 +211,16 @@
         out_shape=[shape((cols, blocks * BLK), BF16), shape((8, blocks * BLK), F32)],
         scratch_shapes=[pltpu.VMEM((cols // HEAD, cols, BLK), BF16)],
         name="attention",
+        cost_estimate=cost(12),
     )(sc, qkvt, kn, qkvt, gq, gkv)
 
 
-def backward_kernel(
-    half, per, first, sc, qt, kn, kt, vn, dot_, ot, lse, gq, gkv, *rest
+def backward_block(
+    half, per, sc, qt, kn, kt, vn, dot_, ot, lse, gq, gkv, dk, dv, zq, zd
 ):
-    if first:
-        dqt, dk_o, dv_o, dk, dv, zq, zd = rest
-    else:
-        dk_i, dv_i, dqt, dk_o, dv_o, dk, dv, zq, zd = rest
     heads = qt.shape[0] // HEAD
-    step = pl.program_id(0)
-    stored, count, at = span(sc, half, per, pl.num_programs(0))
-
-    @pl.when(step == 0)
-    def _():
-        if first:
-            dk[...] = jnp.zeros(dk.shape, F32)
-            dv[...] = jnp.zeros(dv.shape, F32)
-        else:
-            dk[...] = dk_i[...]
-            dv[...] = dv_i[...]
-
+    stored, place, count, at = span(sc, half, per, pl.num_programs(0))
+    queries = gq[:, pl.ds(pl.multiple_of(place * BLK, BLK), BLK)]
     spread(qt, zq)
     spread(dot_, zd)
     deltas = []
@@ -235,8 +230,8 @@
             jnp.sum(dot_[part, :].astype(F32) * ot[part, :].astype(F32), axis=0, keepdims=True)
         )
 
-    def one(start, own):
-        mask = allowed(gkv, gq, start, own)
+    def one(block, start, own):
+        mask = allowed(gkv, queries, block, own)
         keys, values = kn[pl.ds(start, BLK), :], vn[pl.ds(start, BLK), :]
         out = []
         for h in range(heads):
@@ -250,44 +245,128 @@
             out.append(nn(kt[part, at_keys], ds))
         return out
 
-    carry = one(pl.multiple_of(stored * BLK, BLK), True)
+    carry = one(place, pl.multiple_of(stored * BLK, BLK), True)
 
     def body(t, carry):
-        new = one(pl.multiple_of(at(t) * BLK, BLK), False)
+        new = one(*at(t), False)
         return tuple(c + n for c, n in zip(carry, new))
 
-    carry = lax.fori_loop(0, count, body, tuple(carry))
-    for h in range(heads):
-        dqt[h * HEAD : (h + 1) * HEAD, :] = carry[h].astype(BF16)
+    return lax.fori_loop(0, count, body, tuple(carry))
+
+
+def first_back_kernel(per, sc, qt, kn, kt, vn, dot_, ot, lse, gq, gkv, dqt, dk_o, dv_o, dk, dv, zq, zd):
+    step = pl.program_id(0)
+
+    @pl.when(step == 0)
+    def _():
+        dk[...] = jnp.zeros(dk.shape, F32)
+        dv[...] = jnp.zeros(dv.shape, F32)
+
+    dq = backward_block(0, per, sc, qt, kn, kt, vn, dot_, ot, lse, gq, gkv, dk, dv, zq, zd)
+    for h, part in enumerate(dq):
+        dqt[h * HEAD : (h + 1) * HEAD, :] = part.astype(BF16)
 
     @pl.when(step == pl.num_programs(0) - 1)
     def _():
-        dk_o[...] = dk[...].astype(dk_o.dtype)
-        dv_o[...] = dv[...].astype(dv_o.dtype)
-
-
-def attention_back(half, first, sc, qkvt, kn, vn, dout, out, lse, gq, gkv, sums=()):
-    cols3, total = qkvt.shape
-    cols = cols3 // 3
+        dk_o[...] = dk[...]
+        dv_o[...] = dv[...]
+
+
+def folded(v):
+    return sum(v[at : at + FOLD, :] for at in range(0, v.shape[0], FOLD))
+
+
+def halves(row):
+    high = row.astype(BF16)
+    return [high, (row - high.astype(F32)).astype(BF16)]
+
+
+def second_back_kernel(
+    per, pieces, sc, qt, kn, kt, vn, dot_, ot, lse, gq, gkv,
+    dk_i, dv_i, dqa, go, gox, gain, gain_m, n1_h, wt_h, *rest
+):
+    r2, r3, dk_o, dv_o = rest[:4]
+    outs = rest[4 : 4 + pieces]
+    dk, dv, dqb, zq, zd, n1, wt, gs, sems = rest[4 + pieces :]
+    step = pl.program_id(0)
+    cols = dk.shape[0]
+    copies = [
+        pltpu.make_async_copy(n1_h, n1, sems.at[0]),
+        pltpu.make_async_copy(wt_h, wt, sems.at[1]),
+    ]
+
+    @pl.when(step == 0)
+    def _():
+        for copy in copies:
+            copy.start()
+        dk[...] = dk_i[...]
+        dv[...] = dv_i[...]
+
+    dq = backward_block(1, per, sc, qt, kn, kt, vn, dot_, ot, lse, gq, gkv, dk, dv, zq, zd)
+    at = pl.multiple_of(step * BLK, BLK)
+    for h, part in enumerate(dq):
+        dqb[h * HEAD : (h + 1) * HEAD, pl.ds(at, BLK)] = part.astype(BF16)
+
+    @pl.when(step == pl.num_programs(0) - 1)
+    def _():
+        for copy in copies:
+            copy.wait()
+        both = dqb.shape[1]
+        dkb, dvb = dk[...].astype(BF16), dv[...].astype(BF16)
+        dk_o[...] = dkb[:, :both]
+        dv_o[...] = dvb[:, :both]
+        grads = jnp.concatenate([dkb[:, both:], dqb[...], dvb[:, both:]], axis=0)
+        part = nn(grads.T, wt[0 : 3 * cols, :]).astype(BF16)
+        r2[...] = part[: both // 2]
+        r3[...] = part[both // 2 :]
+        gt = [
+            nn(dkb, n1[...]),
+            nn(dqa[...], n1[:both, :]) + nn(dqb[...], n1[both:, :]),
+            nn(dvb, n1[...]),
+        ]
+        total = jnp.zeros((FOLD, gain.shape[1]), F32)
+        for j in range(3):
+            total += folded(gt[j] * wt[j * cols : (j + 1) * cols, :].astype(F32))
+        gain_a = jnp.sum(total, axis=0, keepdims=True) / gain[...]
+        gt.append(go[...] + gox[...].astype(F32))
+        gs[...] = jnp.concatenate(gt, axis=0).T.astype(BF16)
+        depth = gs.shape[0] // pieces
+        extra = halves(gain_a) + halves(jnp.sum(gain_m[...], axis=0, keepdims=True))
+        extra.append(jnp.zeros((EXTRA - len(extra), gain.shape[1]), BF16))
+        extra = jnp.concatenate(extra, axis=0)
+        for j, out in enumerate(outs):
+            start = pl.multiple_of((sc[1] ^ j) * depth, 16) if pieces > 1 else 0
+            out[0:depth, :] = gs[pl.ds(start, depth), :]
+            out[depth : depth + EXTRA, :] = extra
+
+
+def back_specs(half, total, cols):
     blocks = total // BLK // 2
-    per = total // 4 // BLK
-    kind = F32 if first else BF16
-    return pl.pallas_call(
-        functools.partial(backward_kernel, half, per, first),
+    return [
+        SMEM,
+        pl.BlockSpec((cols, BLK), lambda i: (1, half * blocks + i)),
+        whole((total, cols)),
+        pl.BlockSpec((cols, total), lambda i: (0, 0)),
+        whole((total, cols)),
+        pl.BlockSpec((cols, BLK), lambda i: (0, i)),
+        pl.BlockSpec((cols, BLK), lambda i: (0, i)),
+        pl.BlockSpec((8, BLK), lambda i: (0, i)),
+        whole((1, total)),
+        whole((total, 128)),
+    ]
+
+
+def spread_scratch(cols):
+    return [pltpu.VMEM((cols // HEAD, cols, BLK), BF16)] * 2
+
+
+def first_back(sc, qkvt, kn, vn, dout, out, lse, gq, gkv):
+    total, cols = kn.shape
+    blocks = total // BLK // 2
+    return pl.pallas_call(
+        functools.partial(first_back_kernel, total // 4 // BLK),
         grid=(blocks,),
-        in_specs=[
-            SMEM,
-            pl.BlockSpec((cols, BLK), lambda i: (1, half * blocks + i)),
-            whole((total, cols)),
-            pl.BlockSpec((cols, total), lambda i: (0, 0)),
-            whole((total, cols)),
-            pl.BlockSpec((cols, BLK), lambda i: (0, i)),
-            pl.BlockSpec((cols, BLK), lambda i: (0, i)),
-            pl.BlockSpec((8, BLK), lambda i: (0, i)),
-            pl.BlockSpec((1, BLK), lambda i: (0, half * blocks + i)),
-            whole((total, 128)),
-        ]
-        + [whole((cols, total))] * len(sums),
+        in_specs=back_specs(0, total, cols),
         out_specs=[
             pl.BlockSpec((cols, BLK), lambda i: (0, i)),
             whole((cols, total)),
@@ -295,17 +374,48 @@
         ],
         out_shape=[
             shape((cols, blocks * BLK), BF16),
-            shape((cols, total), kind),
-            shape((cols, total), kind),
+            shape((cols, total), F32),
+            shape((cols, total), F32),
         ],
-        scratch_shapes=[
-            pltpu.VMEM((cols, total), F32),
-            pltpu.VMEM((cols, total), F32),
-            pltpu.VMEM((cols // HEAD, cols, BLK), BF16),
-            pltpu.VMEM((cols // HEAD, cols, BLK), BF16),
+        scratch_shapes=[pltpu.VMEM((cols, total), F32)] * 2 + spread_scratch(cols),
+        name="attention_back",
+        cost_estimate=cost(20),
+    )(sc, qkvt, kn, qkvt, vn, dout, out, lse, gq, gkv)
+
+
+def second_back(pieces, sc, qkvt, kn, vn, dout, out, lse, gq, gkv, dk, dv, dqa, go, gox, gain, gain_m, n1, wt):
+    total, cols = kn.shape
+    blocks = total // BLK // 2
+    both = blocks * BLK
+    width = n1.shape[1]
+    piece = (width // pieces + EXTRA, 4 * cols)
+    return pl.pallas_call(
+        functools.partial(second_back_kernel, total // 4 // BLK, pieces),
+        grid=(blocks,),
+        in_specs=back_specs(1, total, cols)
+        + [whole((cols, total))] * 2
+        + [whole((cols, both))]
+        + [whole((cols, width))] * 2
+        + [whole((1, width)), whole(gain_m.shape)]
+        + [pl.BlockSpec(memory_space=pl.ANY)] * 2,
+        out_specs=[whole((both // 2, width))] * 2
+        + [whole((cols, both))] * 2
+        + [whole(piece)] * pieces,
+        out_shape=[shape((both // 2, width), BF16)] * 2
+        + [shape((cols, both), BF16)] * 2
+        + [shape(piece, BF16)] * pieces,
+        scratch_shapes=[pltpu.VMEM((cols, total), F32)] * 2
+        + [pltpu.VMEM((cols, both), BF16)]
+        + spread_scratch(cols)
+        + [
+            pltpu.VMEM(n1.shape, BF16),
+            pltpu.VMEM(wt.shape, BF16),
+            pltpu.VMEM((width, 4 * cols), BF16),
+            pltpu.SemaphoreType.DMA((2,)),
         ],
-        name="attention_back",
-    )(sc, qkvt, kn, qkvt, vn, dout, out, lse, gq, gkv, *sums)
+        name="attention_back_end",
+        cost_estimate=cost(20),
+    )(sc, qkvt, kn, qkvt, vn, dout, out, lse, gq, gkv, dk, dv, dqa, go, gox, gain, gain_m, n1, wt)
 
 
 def out_kernel(om, ox, wm, wx, own, other):
@@ -322,6 +432,7 @@
         out_kernel,
         out_shape=[shape((both // 2, width), F32), shape((both // 2, width), BF16)],
         name="out_projection",
+        cost_estimate=cost(0.01),
     )(om, ox, wm, wx)
 
 
@@ -342,6 +453,7 @@
         out_specs=[tile, tile],
         out_shape=[shape((rows, width), F32), shape((rows, width), BF16)],
         name="middle",
+        cost_estimate=cost(0.01),
     )(tokens, own, got, gain)
 
 
@@ -402,6 +514,7 @@
         out_shape=[shape((rows, width), BF16)] * 4
         + [shape((2 * rows, units), BF16), shape((2 * rows, 2 * units), BF16)],
         name="mlp",
+        cost_estimate=cost(0.01),
     )(na, nb, ya, yb, weights, weights, weights)
 
 
@@ -422,7 +535,7 @@
     def _():
         gain_o[...] = jnp.zeros(gain_o.shape, F32)
 
-    gain_o[...] += jnp.sum(dn2 * h1 * scale, axis=0, keepdims=True)
+    gain_o[...] += folded(dn2 * h1 * scale)
 
 
 def middle_back(dy, h1, a, b, c, gain):
@@ -432,9 +545,10 @@
         middle_back_kernel,
         grid=(4,),
         in_specs=[tile] * 5 + [whole((1, width))],
-        out_specs=[tile, tile, whole((1, width))],
-        out_shape=[shape((rows, width), F32), shape((rows, width), BF16), shape((1, width), F32)],
+        out_specs=[tile, tile, whole((FOLD, width))],
+        out_shape=[shape((rows, width), F32), shape((rows, width), BF16), shape((FOLD, width), F32)],
         name="middle_back",
+        cost_estimate=cost(0.01),
     )(dy, h1, a, b, c, gain)
 
 
@@ -459,6 +573,7 @@
             shape((cols, width), BF16),
         ],
         name="out_back",
+        cost_estimate=cost(0.01),
     )(own, other, wm, wx, om, ox)
 
 
@@ -470,53 +585,15 @@
     b_o[...] = part[rows:]
 
 
-def rows_back(half, dk, dq, dv, wt):
+def rows_back(dk, dq, dv, wt):
     cols, both = dq.shape
     width = wt.shape[1]
-    side = pl.BlockSpec((cols, both), lambda i: (0, half))
     return pl.pallas_call(
         rows_back_kernel,
-        grid=(1,),
-        in_specs=[side, whole((cols, both)), side, whole(wt.shape)],
-        out_specs=[whole((both // 2, width))] * 2,
         out_shape=[shape((both // 2, width), BF16)] * 2,
         name="rows_back",
+        cost_estimate=cost(0.01),
     )(dk, dq, dv, wt)
-
-
-def weights_back_kernel(pieces, sc, dk, dqa, dqb, dv, n1, wt, gain, gain_o, *rest):
-    outs, gs = rest[:pieces], rest[pieces]
-    cols, half = dqa.shape
-    gt = [
-        nn(dk[...], n1[...]),
-        nn(dqa[...], n1[:half, :]) + nn(dqb[...], n1[half:, :]),
-        nn(dv[...], n1[...]),
-    ]
-    total = jnp.zeros(gain.shape, F32)
-    for j in range(3):
-        at = slice(j * cols, (j + 1) * cols)
-        total += jnp.sum(gt[j] * wt[at, :].astype(F32), axis=0, keepdims=True)
-    gain_o[...] = total / gain[...]
-    gs[...] = jnp.concatenate(gt, axis=0).T.astype(BF16)
-    if pieces == 1:
-        outs[0][...] = gs[...]
-    else:
-        depth = outs[0].shape[0]
-        for j in range(pieces):
-            outs[j][...] = gs[pl.ds(pl.multiple_of((sc[1] ^ j) * depth, 16), depth), :]
-
-
-def weights_back(pieces, sc, dk, dqa, dqb, dv, n1, wt, gain):
-    cols, total = dk.shape
-    width = n1.shape[1]
-    return pl.pallas_call(
-        functools.partial(weights_back_kernel, pieces),
-        in_specs=[SMEM] + [pl.BlockSpec(memory_space=pltpu.VMEM)] * 7,
-        out_shape=[shape((1, width), F32)]
-        + [shape((width // pieces, 3 * cols), BF16)] * pieces,
-        scratch_shapes=[pltpu.VMEM((width, 3 * cols), BF16)],
-        name="weights_back",
-    )(sc, dk, dqa, dqb, dv, n1, wt, gain)
 
 
 def last_kernel(tokens, dh1, a, b, c, gain, out):
@@ -541,7 +618,37 @@
         out_specs=tile,
         out_shape=shape((rows, width), BF16),
         name="last",
+        cost_estimate=cost(0.01),
     )(tokens, dh1, a, b, c, gain)
+
+
+def grads_sum_kernel(count, *refs):
+    ins, outs, gains_o = refs[:count], refs[count:-1], refs[-1]
+    rows, cols = outs[0].shape
+    total = ins[0][0:rows, :].astype(F32)
+    for ref in ins[1:]:
+        total = total + ref[0:rows, :].astype(F32)
+    for j, ref in enumerate(outs):
+        ref[...] = total[:, j * cols : (j + 1) * cols]
+    tail = [ref[rows : rows + EXTRA, :].astype(F32) for ref in ins]
+    gains = tail[0]
+    for part in tail[1:]:
+        gains = gains + part
+    gains = gains[0:4, :] + gains[4:8, :]
+    gains_o[...] = jnp.concatenate(
+        [gains[0:1, :] + gains[1:2, :], gains[2:3, :] + gains[3:4, :]], axis=0
+    )
+
+
+def grads_sum(parts):
+    rows, width = parts[0].shape
+    rows -= EXTRA
+    return pl.pallas_call(
+        functools.partial(grads_sum_kernel, len(parts)),
+        out_shape=[shape((rows, width // 4), F32)] * 4 + [shape((2, width), F32)],
+        name="grads_sum",
+        cost_estimate=cost(0.01),
+    )(*parts)
 
 
 def local(
@@ -581,130 +688,119 @@
     gain_a, gain_m = norm_attn[None], norm_mlp[None]
 
     tok2 = across(tokens)
-    tok1 = core(tokens)
     w_attn = jnp.concatenate([w_key, w_query, w_value, w_out], axis=1)
     if direct:
-        w_pieces = [w_attn] + [far(w_attn, k) for k in range(1, dp)]
+        near = [w_attn] + [far(w_attn, k) for k in range(2, dp, 2)]
+        w_pieces = [p for v in near for p in (v, far(v, 1))]
+        tok1 = core(after(tokens, w_pieces[1]))
     else:
         w_pieces = [lax.all_gather(w_attn, "dp", axis=0, tiled=True)]
+        tok1 = core(tokens)
     w_mlp = lax.all_gather(
         jnp.concatenate([w_gate, w_up, w_down], axis=1), "dp", axis=0, tiled=True
     )
-    tok3 = core(tok2)
-
-    ids = group_ids.reshape(4, length // 4)
+    tok3 = core(after(tok2, *w_pieces[1::2]))
+
+    gq = group_ids
+    flat = group_ids[0]
     valid = valid_counts[0]
-    flat = ids.reshape(-1)
     tiles = flat.reshape(length // BLK, BLK)
     low = jnp.sum(flat[None, :] < tiles[:, :1], axis=1) // BLK
     high = jnp.minimum(jnp.sum(flat[None, :] <= tiles[:, -1:], axis=1), valid)
     high = (high + BLK - 1) // BLK
     head = jnp.stack([me, row, valid, valid, valid, valid, valid, valid])
     sc = jnp.concatenate([head, low, high]).astype(jnp.int32)
-    place = jnp.arange(length, dtype=jnp.int32).reshape(4, length // 4)
-    keyed = jnp.where(place < valid, ids, -1)
-
-    def relative(v):
-        v = jnp.where(me % 2 == 1, v[jnp.array([1, 0, 3, 2])], v)
-        return jnp.where(me >= 2, v[jnp.array([2, 3, 0, 1])], v)
-
-    gq = relative(ids).reshape(1, length)
-    gkv = jnp.broadcast_to(relative(keyed).reshape(length, 1), (length, 128))
+    keyed = jnp.where(jnp.arange(length, dtype=jnp.int32) < valid, flat, -1)
+    gkv = jnp.broadcast_to(keyed[:, None], (length, 128))
 
     n1, qkvt, kn, vn, wt = qkv(sc, (tokens, tok1, tok2, tok3), gain_a, w_pieces, cols)
     wo = wt[3 * cols :]
     wo_x = across(wo)
     dy0 = cotangent
-    dy2 = across(after(cotangent, wo))
-    dy1 = core(after(cotangent, wo))
-    dy3 = core(dy2)
+    dy2 = across(after(cotangent, tok2))
+    dy1 = core(after(cotangent, tok3))
 
     o_far, lse_far = attention(1, sc, qkvt, kn, gq, gkv)
-    o_x = across(o_far)
+    o_x = across(after(o_far, dy2))
+    dy3 = core(after(dy2, o_far))
     o_own, lse_own = attention(0, after(sc, o_far), qkvt, kn, gq, gkv)
     p_own, p_other = out_projection(o_own, o_x, wo, wo_x)
     h1, n2 = middle(tokens, p_own, core(p_other), gain_m)
 
     n2_2 = across(n2)
     n2_1 = core(n2)
-    n2_3 = core(n2_2)
     m0, m1, d0, d1, hid_a, dgu_a = mlp_both(n2, n2_1, dy0, dy1, w_mlp)
+    n2_a = jnp.concatenate([n2, n2_1], axis=0)
+    gu_a = tn(n2_a, dgu_a)
+    n2_3 = core(after(n2_2, gu_a))
     m2, m3, d2, d3, hid_b, dgu_b = mlp_both(n2_2, n2_3, dy2, dy3, w_mlp)
 
     def summed(a, b):
         return (a.astype(F32) + b.astype(F32)).astype(BF16)
 
-    d_x = across(summed(d2, core(d3)))
-    dh1, da, gain_m_part = middle_back(dy0, h1, d0, core(d1), d_x, gain_m)
-    m_x = across(summed(after(m2, d_x), core(after(m3, d_x))))
-    output = (
-        h1 + (m0.astype(F32) + core(m1).astype(F32) + m_x.astype(F32))
-    ).astype(BF16)
-    n2_a = jnp.concatenate([n2, n2_1], axis=0)
+    d_sum = summed(d2, core(d3))
+    d_x = across(d_sum)
+    dgu_b, hid_a, hid_b = after((dgu_b, hid_a, hid_b), d_sum)
+    d_core = core(d1)
+    m_sum, m_core = summed(m2, core(m3)), core(m1)
     n2_b = jnp.concatenate([n2_2, n2_3], axis=0)
     dy_a = jnp.concatenate([dy0, dy1], axis=0)
     dy_b = jnp.concatenate([dy2, dy3], axis=0)
-    grad_gu = tn(n2_a, dgu_a) + tn(n2_b, dgu_b)
+    grad_gu = gu_a + tn(n2_b, dgu_b)
     grad_d = tn(dy_a, hid_a) + tn(dy_b, hid_b)
+    mlp_all = jnp.concatenate([grad_gu.astype(BF16), grad_d.astype(BF16)], axis=1)
+    mlp_grads = lax.psum_scatter(mlp_all, "dp", scatter_dimension=0, tiled=True)
+    dh1, da, gain_m_part = middle_back(dy0, h1, d0, d_core, after(d_x, mlp_all, m_sum, m_core), gain_m)
 
     do_own, do_send, go, go_send = out_back(da, core(da), wo, wo_x, o_own, o_x)
     do_far = across(do_send)
-    grad_o = (go + across(go_send).astype(F32)).T
-    mlp_grads = lax.psum_scatter(
-        jnp.concatenate([grad_gu.astype(BF16), grad_d.astype(BF16), grad_o.astype(BF16)], axis=1),
-        "dp",
-        scatter_dimension=0,
-        tiled=True,
-    ).astype(F32)
-
-    dq_own, dk, dv = attention_back(
-        0, True, sc, qkvt, kn, vn, do_own, o_own, lse_own, gq, gkv
+    go_x = across(go_send)
+    dq_own, dk, dv = first_back(sc, qkvt, kn, vn, do_own, o_own, lse_own, gq, gkv)
+    m_x = across(after(m_sum, do_far, go_x))
+    r2, r3, dk_own, dv_own, *grads = second_back(
+        dp if direct else 1,
+        sc, qkvt, kn, vn, do_far, o_far, lse_far, gq, gkv,
+        dk, dv, dq_own, go, go_x, gain_a, gain_m_part, n1, wt,
     )
-    dq_far, dk, dv = attention_back(
-        1, False, sc, qkvt, kn, vn, do_far, o_far, lse_far, gq, gkv, (dk, dv)
-    )
-    r2, r3 = rows_back(1, dk, dq_far, dv, wt)
-    r_x = across(summed(r2, core(r3)))
+    r_sum = summed(r2, core(after(r3, m_x)))
+    r_x = across(r_sum)
+    r0, r1 = rows_back(after(dk_own, r_sum), dq_own, dv_own, wt)
+    grad_tokens = last(tokens, dh1, r0, core(r1), r_x, gain_a)
+    output = (
+        h1 + (m0.astype(F32) + m_core.astype(F32) + after(m_x, r_sum).astype(F32))
+    ).astype(BF16)
+    depth = w_query.shape[0]
     if direct:
-        pieces = dp
-    else:
-        pieces = 1
-    gain_a_part, *grads = weights_back(
-        pieces, sc, after(dk, r2), dq_own, dq_far, dv, n1, wt, gain_a
-    )
-    if direct:
-        attn_grads = grads[0].astype(F32)
-        for k in range(1, dp):
-            attn_grads = attn_grads + far(grads[k], k).astype(F32)
-    else:
-        attn_grads = lax.psum_scatter(
-            grads[0], "dp", scatter_dimension=0, tiled=True
-        ).astype(F32)
-    r0, r1 = rows_back(0, dk, dq_own, dv, wt)
-    grad_tokens = last(tokens, dh1, r0, core(r1), r_x, gain_a)
-
-    gains = jnp.concatenate([gain_a_part, gain_m_part], axis=0)
-    if direct:
+        parts = []
+        for k in range(0, dp, 2):
+            near, other = grads[k], after(far(grads[k + 1], 1), r_sum)
+            both = summed(near[:depth], other[:depth])
+            part = jnp.concatenate([both, near[depth : depth + 4], other[depth : depth + 4]], axis=0)
+            parts.append(part if k == 0 else far(part, k))
+        grad_k, grad_q, grad_v, grad_o, gains = grads_sum(parts)
+        gains = after(gains, r_x)
         gains = gains + core(gains)
         gains = gains + across(gains)
-        k = 1
-        while k < dp:
-            gains = gains + far(gains, k)
-            k *= 2
     else:
-        gains = lax.psum(gains, ("dp", "mp"))
+        width = tokens.shape[1]
+        attn_grads = lax.psum_scatter(
+            grads[0][:width], "dp", scatter_dimension=0, tiled=True
+        ).astype(F32)
+        grad_k, grad_q, grad_v, grad_o = jnp.split(attn_grads, 4, axis=1)
+        extra = grads[0][width : width + 4].astype(F32)
+        gains = lax.psum(extra[0::2] + extra[1::2], ("dp", "mp"))
 
     units = w_gate.shape[1]
     return (
         output,
         grad_tokens,
-        attn_grads[:, cols : 2 * cols],
-        attn_grads[:, :cols],
-        attn_grads[:, 2 * cols :],
-        mlp_grads[:, 3 * units :],
-        mlp_grads[:, :units],
-        mlp_grads[:, units : 2 * units],
-        mlp_grads[:, 2 * units : 3 * units],
+        grad_q,
+        grad_k,
+        grad_v,
+        grad_o,
+        mlp_grads[:, :units].astype(F32),
+        mlp_grads[:, units : 2 * units].astype(F32),
+        mlp_grads[:, 2 * units :].astype(F32),
         gains[0],
         gains[1],
     )

time: 371 us -> 276 us (0.74)
  waiting for transfers between devices: 111 us -> 43.6 us
  starting transfers between devices: 75.5 us -> 44.2 us
  other arithmetic: 13.7 us -> 21.1 us
  matrix products: 15.5 us -> 10.7 us
  Pallas kernels: 121 us -> 125 us
    ppermute x11, waiting for transfers between devices: 69.9 us -> 9.67 us  [across(): return lax.ppermute(v, 'mp', [(i, i ^ 2) for i in range(mp)])]
    ppermute x17 -> x14, starting transfers between devices: 54.5 us -> 24.2 us  [far(): return lax.ppermute(v, 'dp', [(i, i ^ k) for i in range(dp)])]
    ppermute x17 -> x14, waiting for transfers between devices: 38.4 us -> 24 us  [far(): return lax.ppermute(v, 'dp', [(i, i ^ k) for i in range(dp)])]
    ppermute x15, waiting for transfers between devices: 2.81 us -> 9.9 us  [core(): return lax.ppermute(v, 'mp', [(i, i ^ 1) for i in range(mp)])]
    convert_element_type x3 -> x7, other arithmetic: 1.43 us -> 6.89 us  [summed(): return (a.astype(F32) + b.astype(F32)).astype(BF16)]
    dot_general x4, matrix products: 15.5 us -> 10.7 us  [tn(): lax.dot_general(a, b, (((0,), (0,)), ((), ())), preferred_element_type=F32)]
    pallas_call x5 -> x4, Pallas kernels: 48.6 us -> 50.3 us  [the longest x1 24.6 us: second_back(): pl.pallas_call(functools.partial(second_back_kernel, total // 4 // BLK, p...]
    unnamed x104 -> x93, local copies, waits for them, and re-layouts: 9.53 us -> 10.9 us
  transfers between devices with their start and end apart: 45 -> 42, of which waited for: 21 -> 13; matrix products, arithmetic and copies ran while one was open for 10% -> 14% of each run, Pallas kernels for 30% -> 39%
where the time goes in v2:
time: 276 us; the launch traced here: 279 us
  Pallas kernels  125 us (45%)
  starting transfers between devices  44.2 us (16%)
  waiting for transfers between devices  43.6 us (16%)
  other arithmetic  21.1 us (8%)
  local copies, waits for them, and re-layouts  19.4 us (7%)
  between operations  15.3 us (6%)
  matrix products  10.7 us (4%)
    pallas_call x1, Pallas kernels, second_back(): pl.pallas_call(functools.partial(second_back_kernel, total // 4 // BLK, p...  24.6 us
    ppermute x14, starting transfers between devices, far(): return lax.ppermute(v, 'dp', [(i, i ^ k) for i in range(dp)])  24.2 us
    ppermute x14, waiting for transfers between devices, far(): return lax.ppermute(v, 'dp', [(i, i ^ k) for i in range(dp)])  24 us
    pallas_call x2, Pallas kernels, attention(): pl.pallas_call(functools.partial(forward_kernel, half, per), grid=(blocks...  23.4 us
    pallas_call x2, Pallas kernels, mlp_both(): pl.pallas_call(mlp_kernel, grid=(2 * per,), in_specs=[first, second, firs...  20.9 us
    pallas_call x1, Pallas kernels, first_back(): pl.pallas_call(functools.partial(first_back_kernel, total // 4 // BLK), g...  19.5 us
    ppermute x11, starting transfers between devices, across(): return lax.ppermute(v, 'mp', [(i, i ^ 2) for i in range(mp)])  17.9 us
    unnamed x93, local copies, waits for them, and re-layouts  10.9 us
  transfers between devices with their start and end apart: 42, of which 13 were waited for; matrix products, arithmetic and copies ran while one was open for 14% of the time, Pallas kernels for 39%

profile of v2, /device:TPU:0, one launch (start us, length us, event | category | flops | bytes accessed | tf_op | source)
XLA Modules:
  0.0 279.3 jit_solution(8848695865678877589)
XLA Ops:
  7.2 3.0 %collective-permute-start.2 = (bf16[512,768]{1,0:T(8,128)(2,1)}, bf16[512,768]{1,0:T(8,128)(2,1)S(1)}, u32[]{:S(2)}, u32[]{:S(2)}) collective-permute-start(bf16[512,768]{1,0:T(8,128)(2,1)} %tokens.3), channel_id=1, source_target_pairs={{0,2},{1,3},{2,0},{3,1},{4,6},{5,7},{6,4},{7,5},{8,10},{9,11},{10,... | collective-permute-start | bytes 2359304 | tf_op jit(solution)/shard_map/ppermute | solution.py:679
  11.2 3.7 %collective-permute-start.7 = (bf16[96,768]{1,0:T(8,128)(2,1)S(1)}, bf16[96,768]{1,0:T(8,128)(2,1)S(1)}, u32[]{:S(2)}, u32[]{:S(2)}) collective-permute-start(bf16[96,768]{1,0:T(8,128)(2,1)S(1)} %pad_maximum_fusion.6.rest_0_), channel_id=1, source_target_pairs={{0,24},{4,28},{8,16},{12,20},{16,8},{20,12},{24,0},{28,4},{1,25},{... | collective-permute-start | bytes 442376 | tf_op jit(solution)/shard_map/ppermute | solution.py:682
  17.2 2.7 collective-permute-done.7.rest_6_
  21.4 5.7 %collective-permute-done.5.rest_4_ = bf16[96,768]{1,0:T(8,128)(2,1)S(1)} collective-permute-done((bf16[96,768]{1,0:T(8,128)(2,1)S(1)}, bf16[96,768]{1,0:T(8,128)(2,1)S(1)}, u32[]{:S(2)}, u32[]{:S(2)}) %collective-permute-start.5) | collective-permute-done | bytes 147488 | tf_op jit(solution)/shard_map/ppermute | solution.py:682
  41.9 9.4 %qkv.1 = (bf16[2048,768]{1,0:T(8,128)(2,1)}, bf16[576,2048]{1,0:T(8,128)(2,1)}, bf16[2048,192]{1,0:T(8,128)(2,1)}, bf16[2048,192]{1,0:T(8,128)(2,1)}, bf16[768,768]{1,0:T(8,128)(2,1)}) custom-call(s32[24]{0:T(128)} %concatenate.36.sc, bf16[512,768]{1,0:T(8,128)(2,1)} %tokens.3, bf16[512,768]{1,0:T(8,128)(2,1)} %copy-done.15, bf16[512,768]{1,0:T(8,128)(2,1)} %copy-done.10, ...), custom_call_target="tpu_custom_call" | custom-call | flops 10000000 | bytes 1024 | tf_op jit(solution)/shard_map/qkv/pallas_call | solution.py:78
  55.1 11.7 %attention.2 = (bf16[192,1024]{1,0:T(8,128)(2,1)}, f32[8,1024]{1,0:T(8,128)}) custom-call(s32[24]{0:T(128)} %concatenate.36.sc, bf16[576,2048]{1,0:T(8,128)(2,1)} %get-tuple-element.88.qt.vt.kt, bf16[2048,192]{1,0:T(8,128)(2,1)} %get-tuple-element.89.kn, bf16[576,2048]{1,0:T(8,128)(2,1)} %get-tuple-element.88.qt.vt.kt, s32[1,2048]{1,0:T(1,128)} %gq.7, ...), custom_call_target="tpu_custom_call" | custom-call | flops 12000000000 | bytes 1024 | tf_op jit(solution)/shard_map/attention/pallas_call | solution.py:196
  67.5 11.7 %attention.3 = (bf16[192,1024]{1,0:T(8,128)(2,1)}, f32[8,1024]{1,0:T(8,128)}) custom-call(s32[24]{0:T(128)} %concatenate.36.sc, bf16[576,2048]{1,0:T(8,128)(2,1)} %get-tuple-element.88.qt.vt.kt, bf16[2048,192]{1,0:T(8,128)(2,1)} %get-tuple-element.89.kn, bf16[576,2048]{1,0:T(8,128)(2,1)} %get-tuple-element.88.qt.vt.kt, s32[1,2048]{1,0:T(1,128)} %gq.7, ...), custom_call_target="tpu_custom_call" | custom-call | flops 12000000000 | bytes 1024 | tf_op jit(solution)/shard_map/attention/pallas_call | solution.py:196
  80.0 3.6 %out_projection.1 = (f32[512,768]{1,0:T(8,128)}, bf16[512,768]{1,0:T(8,128)(2,1)}) custom-call(bf16[192,1024]{1,0:T(8,128)(2,1)} %get-tuple-element.92.om.ot, bf16[192,1024]{1,0:T(8,128)(2,1)} %copy-done.4, bf16[192,768]{1,0:T(8,128)(2,1)} %copy-done.3, bf16[192,768]{1,0:T(8,128)(2,1)} %copy-done.5), custom_call_target="tpu_custom_call" | custom-call | flops 10000000 | bytes 1024 | tf_op jit(solution)/shard_map/out_projection/pallas_call | solution.py:431
  86.9 4.1 %middle.1 = (f32[512,768]{1,0:T(8,128)}, bf16[512,768]{1,0:T(8,128)(2,1)}) custom-call(bf16[512,768]{1,0:T(8,128)(2,1)} %tokens.3, f32[512,768]{1,0:T(8,128)} %get-tuple-element.96.own, bf16[512,768]{1,0:T(8,128)(2,1)} %copy-done.23, f32[1,768]{1,0:T(1,128)} %broadcast_in_dim.19.gain), custom_call_target="tpu_custom_call" | custom-call | flops 10000000 | bytes 1024 | tf_op jit(solution)/shard_map/middle/pallas_call | solution.py:449
  93.7 10.5 %mlp.2 = (bf16[512,768]{1,0:T(8,128)(2,1)}, bf16[512,768]{1,0:T(8,128)(2,1)}, bf16[512,768]{1,0:T(8,128)(2,1)}, bf16[512,768]{1,0:T(8,128)(2,1)}, bf16[1024,512]{1,0:T(8,128)(2,1)}, /*index=5*/bf16[1024,1024]{1,0:T(8,128)(2,1)}) custom-call(bf16[512,768]{1,0:T(8,128)(2,1)} %get-tuple-element.99.na, bf16[512,768]{1,0:T(8,128)(2,1)} %collective-permute-done.14.nb, ...), custom_call_target="tpu_custom_call" | custom-call | flops 10000000 | bytes 1024 | tf_op jit(solution)/shard_map/mlp/pallas_call | solution.py:502
  104.1 5.6 %fusion = f32[768,1024]{1,0:T(8,128)} fusion(bf16[1024,1024]{1,0:T(8,128)(2,1)} %get-tuple-element.103, bf16[512,768]{1,0:T(8,128)(2,1)} %collective-permute-done.14.nb, bf16[512,768]{1,0:T(8,128)(2,1)} %get-tuple-element.99.na), kind=kOutput, calls=%fused_computation.2 | convolution fusion | flops 1613758464 | bytes 6815744 | tf_op jit(solution)/shard_map/dot_general | solution.py:30
  111.2 2.3 collective-permute-done.18.nb
  114.4 10.4 %mlp.3 = (bf16[512,768]{1,0:T(8,128)(2,1)}, bf16[512,768]{1,0:T(8,128)(2,1)}, bf16[512,768]{1,0:T(8,128)(2,1)}, bf16[512,768]{1,0:T(8,128)(2,1)}, bf16[1024,512]{1,0:T(8,128)(2,1)}, /*index=5*/bf16[1024,1024]{1,0:T(8,128)(2,1)}) custom-call(bf16[512,768]{1,0:T(8,128)(2,1)} %copy-done.13, bf16[512,768]{1,0:T(8,128)(2,1)} %copy-done.17, ...), custom_call_target="tpu_custom_call" | custom-call | flops 10000000 | bytes 1024 | tf_op jit(solution)/shard_map/mlp/pallas_call | solution.py:502
  127.3 2.2 add_convert_fusion.4
  131.1 2.3 fusion.11
  141.2 8.2 %collective-permute-done.23.c = bf16[512,768]{1,0:T(8,128)(2,1)S(1)} collective-permute-done((bf16[512,768]{1,0:T(8,128)(2,1)}, bf16[512,768]{1,0:T(8,128)(2,1)S(1)}, u32[]{:S(2)}, u32[]{:S(2)}) %collective-permute-start.23) | collective-permute-done | bytes 786464 | tf_op jit(solution)/shard_map/ppermute | solution.py:679
  150.5 4.8 %middle_back.1 = (f32[512,768]{1,0:T(8,128)}, bf16[512,768]{1,0:T(8,128)(2,1)}, f32[32,768]{1,0:T(8,128)}) custom-call(bf16[512,768]{1,0:T(8,128)(2,1)} %dy.1, f32[512,768]{1,0:T(8,128)} %get-tuple-element.98.h1_r, bf16[512,768]{1,0:T(8,128)(2,1)} %get-tuple-element.108.a, bf16[512,768]{1,0:T(8,128)(2,1)} %copy-done.19, bf16[512,768]{1,0:T(8,128)(2,1)} %copy-done.20, ...), custom_call_target="tpu_custom_call" | custom-call | flops 10000000 | bytes 1024 | tf_op jit(solution)/shard_map/middle_back/pallas_call | solution.py:544
  155.4 2.5 collective-permute-done.24.other
  158.7 4.3 %out_back.1 = (bf16[192,1024]{1,0:T(8,128)(2,1)}, bf16[192,1024]{1,0:T(8,128)(2,1)}, f32[192,768]{1,0:T(8,128)}, bf16[192,768]{1,0:T(8,128)(2,1)}) custom-call(bf16[512,768]{1,0:T(8,128)(2,1)} %get-tuple-element.119.own, bf16[512,768]{1,0:T(8,128)(2,1)} %copy-done.22, bf16[192,768]{1,0:T(8,128)(2,1)} %copy-done.3, bf16[192,768]{1,0:T(8,128)(2,1)} %copy-done.5, ...), custom_call_target="tpu_custom_call" | custom-call | flops 10000000 | bytes 1024 | tf_op jit(solution)/shard_map/out_back/pallas_call | solution.py:567
  165.0 19.5 %attention_back.1 = (bf16[192,1024]{1,0:T(8,128)(2,1)}, f32[192,2048]{1,0:T(8,128)}, f32[192,2048]{1,0:T(8,128)}) custom-call(s32[24]{0:T(128)} %concatenate.36.sc, bf16[576,2048]{1,0:T(8,128)(2,1)} %get-tuple-element.88.qt.vt.kt, bf16[2048,192]{1,0:T(8,128)(2,1)} %get-tuple-element.89.kn, bf16[576,2048]{1,0:T(8,128)(2,1)} %get-tuple-element.88.qt.vt.kt, ...), custom_call_target="tpu_custom_call" | custom-call | flops 20000000000 | bytes 1024 | tf_op jit(solution)/shard_map/attention_back/pallas_call | solution.py:366
  186.2 24.6 %attention_back_end.1 = (bf16[512,768]{1,0:T(8,128)(2,1)}, bf16[512,768]{1,0:T(8,128)(2,1)}, bf16[192,1024]{1,0:T(8,128)(2,1)}, bf16[192,1024]{1,0:T(8,128)(2,1)...) custom-call(s32[24]{0:T(128)} %concatenate.36.sc, ...), custom_call_target="tpu_custom_call" | custom-call | flops 20000000000 | bytes 1024 | tf_op jit(solution)/shard_map/attention_back_end/pallas_call | solution.py:392
  213.8 2.1 collective-permute-start.32
  215.9 2.0 collective-permute-start.36
  217.9 2.2 add_convert_fusion.2
  220.8 9.8 %collective-permute-done.36 = bf16[104,768]{1,0:T(8,128)(2,1)S(1)} collective-permute-done((bf16[104,768]{1,0:T(8,128)(2,1)}, bf16[104,768]{1,0:T(8,128)(2,1)S(1)}, u32[]{:S(2)}, u32[]{:S(2)}) %collective-permute-start.36) | collective-permute-done | bytes 159776 | tf_op jit(solution)/shard_map/ppermute | solution.py:682
  231.5 8.1 %collective-permute-start.33 = (bf16[104,768]{1,0:T(8,128)(2,1)}, bf16[104,768]{1,0:T(8,128)(2,1)S(1)}, u32[]{:S(2)}, u32[]{:S(2)}) collective-permute-start(bf16[104,768]{1,0:T(8,128)(2,1)} %pad_maximum_fusion.3), channel_id=1, source_target_pairs={{0,8},{4,12},{8,0},{12,4},{16,24},{20,28},{24,16},{28,20},{1,9},{5... | collective-permute-start | bytes 479240 | tf_op jit(solution)/shard_map/ppermute | solution.py:682
  240.3 4.3 %rows_back.1 = (bf16[512,768]{1,0:T(8,128)(2,1)}, bf16[512,768]{1,0:T(8,128)(2,1)}) custom-call(bf16[192,1024]{1,0:T(8,128)(2,1)} %get-tuple-element.139.dk, bf16[192,1024]{1,0:T(8,128)(2,1)} %get-tuple-element.129.dqa.dq, bf16[192,1024]{1,0:T(8,128)(2,1)} %get-tuple-element.140.dv, bf16[768,768]{1,0:T(8,128)(2,1)} %get-tuple-element.95.wt_h.wt), custom_call_target="tpu_custom_call" | custom-call | flops 10000000 | bytes 1024 | tf_op jit(solution)/shard_map/rows_back/pallas_call | solution.py:591
  245.8 2.4 collective-permute-start.37
  250.0 4.3 %collective-permute-done.37.refs_3_ = bf16[104,768]{1,0:T(8,128)(2,1)} collective-permute-done((bf16[104,768]{1,0:T(8,128)(2,1)S(1)}, bf16[104,768]{1,0:T(8,128)(2,1)}, u32[]{:S(2)}, u32[]{:S(2)}) %collective-permute-start.37) | collective-permute-done | bytes 159776 | tf_op jit(solution)/shard_map/ppermute | solution.py:682
  258.3 4.9 %collective-permute-start.39 = (f32[2,768]{1,0:T(2,128)S(1)}, f32[2,768]{1,0:T(2,128)S(1)}, u32[]{:S(2)}, u32[]{:S(2)}) collective-permute-start(f32[2,768]{1,0:T(2,128)S(1)} %add.62), channel_id=1, source_target_pairs={{0,2},{1,3},{2,0},{3,1},{4,6},{5,7},{6,4},{7,5},{8,10},{9,11},{10,... | collective-permute-start | bytes 18440 | tf_op jit(solution)/shard_map/ppermute | solution.py:679
  263.2 2.3 add_convert_fusion.1
  265.6 4.4 %last.1 = bf16[512,768]{1,0:T(8,128)(2,1)} custom-call(bf16[512,768]{1,0:T(8,128)(2,1)} %tokens.3, f32[512,768]{1,0:T(8,128)} %get-tuple-element.137.dh1, bf16[512,768]{1,0:T(8,128)(2,1)} %get-tuple-element.141.a, bf16[512,768]{1,0:T(8,128)(2,1)} %collective-permute-done.29.b, bf16[512,768]{1,0:T(8,128)(2,1)} %collective-permute-done.30.c, ...), custom_call_target="tpu_custom_call" | custom-call | flops 10000000 | bytes 1024 | tf_op jit(solution)/shard_map/last/pallas_call | solution.py:614
  (205 shorter events, 64.8 us)
Async XLA Ops:
  7.2 86.5 %all-gather.2.cloned.1.call-start = ((), (), s32[]{:S(2)}) async-start(), calls=%async_computation.1 | async-start | bytes 2654208 | tf_op jit(solution)/shard_map/all_gather | solution.py:699
  7.2 28.5 %collective-permute-start.2 = (bf16[512,768]{1,0:T(8,128)(2,1)}, bf16[512,768]{1,0:T(8,128)(2,1)S(1)}, u32[]{:S(2)}, u32[]{:S(2)}) collective-permute-start(bf16[512,768]{1,0:T(8,128)(2,1)} %tokens.3), channel_id=1, source_target_pairs={{0,2},{1,3},{2,0},{3,1},{4,6},{5,7},{6,4},{7,5},{8,10},{9,11},{10,... | collective-permute-start | bytes 2359304 | tf_op jit(solution)/shard_map/ppermute | solution.py:679
  11.2 8.7 %collective-permute-start.7 = (bf16[96,768]{1,0:T(8,128)(2,1)S(1)}, bf16[96,768]{1,0:T(8,128)(2,1)S(1)}, u32[]{:S(2)}, u32[]{:S(2)}) collective-permute-start(bf16[96,768]{1,0:T(8,128)(2,1)S(1)} %pad_maximum_fusion.6.rest_0_), channel_id=1, source_target_pairs={{0,24},{4,28},{8,16},{12,20},{16,8},{20,12},{24,0},{28,4},{1,25},{... | collective-permute-start | bytes 442376 | tf_op jit(solution)/shard_map/ppermute | solution.py:682
  14.9 12.2 %collective-permute-start.5 = (bf16[96,768]{1,0:T(8,128)(2,1)S(1)}, bf16[96,768]{1,0:T(8,128)(2,1)S(1)}, u32[]{:S(2)}, u32[]{:S(2)}) collective-permute-start(bf16[96,768]{1,0:T(8,128)(2,1)S(1)} %pad_maximum_fusion.6.rest_0_), channel_id=1, source_target_pairs={{0,16},{4,20},{8,24},{12,28},{16,0},{20,4},{24,8},{28,12},{1,17},{... | collective-permute-start | bytes 442376 | tf_op jit(solution)/shard_map/ppermute | solution.py:682
  14.9 13.7 %collective-permute-start.3 = (bf16[96,768]{1,0:T(8,128)(2,1)S(1)}, bf16[96,768]{1,0:T(8,128)(2,1)S(1)}, u32[]{:S(2)}, u32[]{:S(2)}) collective-permute-start(bf16[96,768]{1,0:T(8,128)(2,1)S(1)} %pad_maximum_fusion.6.rest_0_), channel_id=1, source_target_pairs={{0,8},{4,12},{8,0},{12,4},{16,24},{20,28},{24,16},{28,20},{1,9},{5... | collective-permute-start | bytes 442376 | tf_op jit(solution)/shard_map/ppermute | solution.py:682
  15.7 17.8 %collective-permute-start = (bf16[96,768]{1,0:T(8,128)(2,1)S(1)}, bf16[96,768]{1,0:T(8,128)(2,1)S(1)}, u32[]{:S(2)}, u32[]{:S(2)}) collective-permute-start(bf16[96,768]{1,0:T(8,128)(2,1)S(1)} %pad_maximum_fusion.6.rest_0_), channel_id=1, source_target_pairs={{0,4},{4,0},{8,12},{12,8},{16,20},{20,16},{24,28},{28,24},{1,5},{5... | collective-permute-start | bytes 442376 | tf_op jit(solution)/shard_map/ppermute | solution.py:682
  19.9 13.7 %collective-permute-start.8 = (bf16[96,768]{1,0:T(8,128)(2,1)S(1)}, bf16[96,768]{1,0:T(8,128)(2,1)S(1)}, u32[]{:S(2)}, u32[]{:S(2)}) collective-permute-start(bf16[96,768]{1,0:T(8,128)(2,1)S(1)} %collective-permute-done.7.rest_6_), channel_id=1, source_target_pairs={{0,4},{4,0},{8,12},{12,8},{16,20},{20,16},{24,28},{28,24},{1,5},{5... | collective-permute-start | bytes 442376 | tf_op jit(solution)/shard_map/ppermute | solution.py:682
  30.9 239.8 %reduce-scatter.2.cloned.1.call-start = ((), (), s32[]{:S(2)}) async-start(), calls=%async_computation.2 | async-start | bytes 2654208 | tf_op jit(solution)/shard_map/reduce_scatter | solution.py:752
  39.6 27.2 %collective-permute-start.10 = (bf16[512,768]{1,0:T(8,128)(2,1)}, bf16[512,768]{1,0:T(8,128)(2,1)S(1)}, u32[]{:S(2)}, u32[]{:S(2)}) collective-permute-start(bf16[512,768]{1,0:T(8,128)(2,1)} %dy.1), channel_id=1, source_target_pairs={{0,2},{1,3},{2,0},{3,1},{4,6},{5,7},{6,4},{7,5},{8,10},{9,11},{10,... | collective-permute-start | bytes 2359304 | tf_op jit(solution)/shard_map/ppermute | solution.py:679
  52.3 26.9 %collective-permute-start.12 = (bf16[192,768]{1,0:T(8,128)(2,1)S(1)}, bf16[192,768]{1,0:T(8,128)(2,1)S(1)}, u32[]{:S(2)}, u32[]{:S(2)}) collective-permute-start(bf16[192,768]{1,0:T(8,128)(2,1)S(1)} %slice.74.wm), channel_id=1, source_target_pairs={{0,2},{1,3},{2,0},{3,1},{4,6},{5,7},{6,4},{7,5},{8,10},{9,11},{10,... | collective-permute-start | bytes 884744 | tf_op jit(solution)/shard_map/ppermute | solution.py:679
  66.9 12.3 %collective-permute-start.11 = (bf16[192,1024]{1,0:T(8,128)(2,1)}, bf16[192,1024]{1,0:T(8,128)(2,1)S(1)}, u32[]{:S(2)}, u32[]{:S(2)}) collective-permute-start(bf16[192,1024]{1,0:T(8,128)(2,1)} %get-tuple-element.94.ot), channel_id=1, source_target_pairs={{0,2},{1,3},{2,0},{3,1},{4,6},{5,7},{6,4},{7,5},{8,10},{9,11},{10,... | collective-permute-start | bytes 1179656 | tf_op jit(solution)/shard_map/ppermute | solution.py:679
  84.2 8.6 %collective-permute-start.15 = (bf16[512,768]{1,0:T(8,128)(2,1)S(1)}, bf16[512,768]{1,0:T(8,128)(2,1)S(1)}, u32[]{:S(2)}, u32[]{:S(2)}) collective-permute-start(bf16[512,768]{1,0:T(8,128)(2,1)S(1)} %copy-done.1), channel_id=1, source_target_pairs={{0,1},{1,0},{2,3},{3,2},{4,5},{5,4},{6,7},{7,6},{8,9},{9,8},{10,11... | collective-permute-start | bytes 2359304 | tf_op jit(solution)/shard_map/ppermute | solution.py:676
  91.2 20.0 %collective-permute-start.17 = (bf16[512,768]{1,0:T(8,128)(2,1)}, bf16[512,768]{1,0:T(8,128)(2,1)S(1)}, u32[]{:S(2)}, u32[]{:S(2)}) collective-permute-start(bf16[512,768]{1,0:T(8,128)(2,1)} %get-tuple-element.99.na), channel_id=1, source_target_pairs={{0,2},{1,3},{2,0},{3,1},{4,6},{5,7},{6,4},{7,5},{8,10},{9,11},{10,... | collective-permute-start | bytes 2359304 | tf_op jit(solution)/shard_map/ppermute | solution.py:679
  92.7 18.5 %collective-permute-start.19 = (bf16[512,768]{1,0:T(8,128)(2,1)S(1)}, bf16[512,768]{1,0:T(8,128)(2,1)}, u32[]{:S(2)}, u32[]{:S(2)}) collective-permute-start(bf16[512,768]{1,0:T(8,128)(2,1)S(1)} %collective-permute-done.10.ya), channel_id=1, source_target_pairs={{0,1},{1,0},{2,3},{3,2},{4,5},{5,4},{6,7},{7,6},{8,9},{9,8},{10,11... | collective-permute-start | bytes 2359304 | tf_op jit(solution)/shard_map/ppermute | solution.py:676
  125.0 8.4 %collective-permute-start.20 = (bf16[512,768]{1,0:T(8,128)(2,1)}, bf16[512,768]{1,0:T(8,128)(2,1)S(1)}, u32[]{:S(2)}, u32[]{:S(2)}) collective-permute-start(bf16[512,768]{1,0:T(8,128)(2,1)} %get-tuple-element.107), channel_id=1, source_target_pairs={{0,1},{1,0},{2,3},{3,2},{4,5},{5,4},{6,7},{7,6},{8,9},{9,8},{10,11... | collective-permute-start | bytes 2359304 | tf_op jit(solution)/shard_map/ppermute | solution.py:676
  125.4 15.9 %collective-permute-start.16 = (bf16[512,768]{1,0:T(8,128)(2,1)}, bf16[512,768]{1,0:T(8,128)(2,1)S(1)}, u32[]{:S(2)}, u32[]{:S(2)}) collective-permute-start(bf16[512,768]{1,0:T(8,128)(2,1)} %get-tuple-element.102), channel_id=1, source_target_pairs={{0,1},{1,0},{2,3},{3,2},{4,5},{5,4},{6,7},{7,6},{8,9},{9,8},{10,11... | collective-permute-start | bytes 2359304 | tf_op jit(solution)/shard_map/ppermute | solution.py:676
  125.5 23.9 %collective-permute-start.21 = (bf16[512,768]{1,0:T(8,128)(2,1)}, bf16[512,768]{1,0:T(8,128)(2,1)S(1)}, u32[]{:S(2)}, u32[]{:S(2)}) collective-permute-start(bf16[512,768]{1,0:T(8,128)(2,1)} %get-tuple-element.109), channel_id=1, source_target_pairs={{0,1},{1,0},{2,3},{3,2},{4,5},{5,4},{6,7},{7,6},{8,9},{9,8},{10,11... | collective-permute-start | bytes 2359304 | tf_op jit(solution)/shard_map/ppermute | solution.py:676
  129.6 19.8 %collective-permute-start.23 = (bf16[512,768]{1,0:T(8,128)(2,1)}, bf16[512,768]{1,0:T(8,128)(2,1)S(1)}, u32[]{:S(2)}, u32[]{:S(2)}) collective-permute-start(bf16[512,768]{1,0:T(8,128)(2,1)} %add_convert_fusion.4), channel_id=1, source_target_pairs={{0,2},{1,3},{2,0},{3,1},{4,6},{5,7},{6,4},{7,5},{8,10},{9,11},{10,... | collective-permute-start | bytes 2359304 | tf_op jit(solution)/shard_map/ppermute | solution.py:679
  163.0 21.5 %collective-permute-start.26 = (bf16[192,768]{1,0:T(8,128)(2,1)}, bf16[192,768]{1,0:T(8,128)(2,1)S(1)}, u32[]{:S(2)}, u32[]{:S(2)}) collective-permute-start(bf16[192,768]{1,0:T(8,128)(2,1)} %get-tuple-element.121), channel_id=1, source_target_pairs={{0,2},{1,3},{2,0},{3,1},{4,6},{5,7},{6,4},{7,5},{8,10},{9,11},{10,... | collective-permute-start | bytes 884744 | tf_op jit(solution)/shard_map/ppermute | solution.py:679
  164.5 20.0 %collective-permute-start.25 = (bf16[192,1024]{1,0:T(8,128)(2,1)}, bf16[192,1024]{1,0:T(8,128)(2,1)S(1)}, u32[]{:S(2)}, u32[]{:S(2)}) collective-permute-start(bf16[192,1024]{1,0:T(8,128)(2,1)} %get-tuple-element.120), channel_id=1, source_target_pairs={{0,2},{1,3},{2,0},{3,1},{4,6},{5,7},{6,4},{7,5},{8,10},{9,11},{10,... | collective-permute-start | bytes 1179656 | tf_op jit(solution)/shard_map/ppermute | solution.py:679
  184.6 26.2 %collective-permute-start.27 = (bf16[512,768]{1,0:T(8,128)(2,1)S(1)}, bf16[512,768]{1,0:T(8,128)(2,1)S(1)}, u32[]{:S(2)}, u32[]{:S(2)}) collective-permute-start(bf16[512,768]{1,0:T(8,128)(2,1)S(1)} %add_convert_fusion.5), channel_id=1, source_target_pairs={{0,2},{1,3},{2,0},{3,1},{4,6},{5,7},{6,4},{7,5},{8,10},{9,11},{10,... | collective-permute-start | bytes 2359304 | tf_op jit(solution)/shard_map/ppermute | solution.py:679
  210.8 7.1 %collective-permute-start.28 = (bf16[512,768]{1,0:T(8,128)(2,1)}, bf16[512,768]{1,0:T(8,128)(2,1)S(1)}, u32[]{:S(2)}, u32[]{:S(2)}) collective-permute-start(bf16[512,768]{1,0:T(8,128)(2,1)} %get-tuple-element.135), channel_id=1, source_target_pairs={{0,1},{1,0},{2,3},{3,2},{4,5},{5,4},{6,7},{7,6},{8,9},{9,8},{10,11... | collective-permute-start | bytes 2359304 | tf_op jit(solution)/shard_map/ppermute | solution.py:676
  213.8 16.9 %collective-permute-start.31 = (bf16[104,768]{1,0:T(8,128)(2,1)}, bf16[104,768]{1,0:T(8,128)(2,1)S(1)}, u32[]{:S(2)}, u32[]{:S(2)}) collective-permute-start(bf16[104,768]{1,0:T(8,128)(2,1)} %get-tuple-element.144), channel_id=1, source_target_pairs={{0,4},{4,0},{8,12},{12,8},{16,20},{20,16},{24,28},{28,24},{1,5},{5... | collective-permute-start | bytes 479240 | tf_op jit(solution)/shard_map/ppermute | solution.py:682
  213.8 16.9 %collective-permute-start.32 = (bf16[104,768]{1,0:T(8,128)(2,1)}, bf16[104,768]{1,0:T(8,128)(2,1)S(1)}, u32[]{:S(2)}, u32[]{:S(2)}) collective-permute-start(bf16[104,768]{1,0:T(8,128)(2,1)} %get-tuple-element.147), channel_id=1, source_target_pairs={{0,4},{4,0},{8,12},{12,8},{16,20},{20,16},{24,28},{28,24},{1,5},{5... | collective-permute-start | bytes 479240 | tf_op jit(solution)/shard_map/ppermute | solution.py:682
  215.9 14.8 %collective-permute-start.34 = (bf16[104,768]{1,0:T(8,128)(2,1)}, bf16[104,768]{1,0:T(8,128)(2,1)S(1)}, u32[]{:S(2)}, u32[]{:S(2)}) collective-permute-start(bf16[104,768]{1,0:T(8,128)(2,1)} %get-tuple-element.150), channel_id=1, source_target_pairs={{0,4},{4,0},{8,12},{12,8},{16,20},{20,16},{24,28},{28,24},{1,5},{5... | collective-permute-start | bytes 479240 | tf_op jit(solution)/shard_map/ppermute | solution.py:682
  215.9 14.8 %collective-permute-start.36 = (bf16[104,768]{1,0:T(8,128)(2,1)}, bf16[104,768]{1,0:T(8,128)(2,1)S(1)}, u32[]{:S(2)}, u32[]{:S(2)}) collective-permute-start(bf16[104,768]{1,0:T(8,128)(2,1)} %get-tuple-element.153), channel_id=1, source_target_pairs={{0,4},{4,0},{8,12},{12,8},{16,20},{20,16},{24,28},{28,24},{1,5},{5... | collective-permute-start | bytes 479240 | tf_op jit(solution)/shard_map/ppermute | solution.py:682
  220.1 36.1 %collective-permute-start.30 = (bf16[512,768]{1,0:T(8,128)(2,1)}, bf16[512,768]{1,0:T(8,128)(2,1)}, u32[]{:S(2)}, u32[]{:S(2)}) collective-permute-start(bf16[512,768]{1,0:T(8,128)(2,1)} %add_convert_fusion.2), channel_id=1, source_target_pairs={{0,2},{1,3},{2,0},{3,1},{4,6},{5,7},{6,4},{7,5},{8,10},{9,11},{10,... | collective-permute-start | bytes 2359304 | tf_op jit(solution)/shard_map/ppermute | solution.py:679
  231.5 18.4 %collective-permute-start.33 = (bf16[104,768]{1,0:T(8,128)(2,1)}, bf16[104,768]{1,0:T(8,128)(2,1)S(1)}, u32[]{:S(2)}, u32[]{:S(2)}) collective-permute-start(bf16[104,768]{1,0:T(8,128)(2,1)} %pad_maximum_fusion.3), channel_id=1, source_target_pairs={{0,8},{4,12},{8,0},{12,4},{16,24},{20,28},{24,16},{28,20},{1,9},{5... | collective-permute-start | bytes 479240 | tf_op jit(solution)/shard_map/ppermute | solution.py:682
  240.3 9.6 %collective-permute-start.35 = (bf16[104,768]{1,0:T(8,128)(2,1)}, bf16[104,768]{1,0:T(8,128)(2,1)S(1)}, u32[]{:S(2)}, u32[]{:S(2)}) collective-permute-start(bf16[104,768]{1,0:T(8,128)(2,1)} %pad_maximum_fusion.4), channel_id=1, source_target_pairs={{0,16},{4,20},{8,24},{12,28},{16,0},{20,4},{24,8},{28,12},{1,17},{... | collective-permute-start | bytes 479240 | tf_op jit(solution)/shard_map/ppermute | solution.py:682
  244.6 21.0 %collective-permute-start.29 = (bf16[512,768]{1,0:T(8,128)(2,1)}, bf16[512,768]{1,0:T(8,128)(2,1)}, u32[]{:S(2)}, u32[]{:S(2)}) collective-permute-start(bf16[512,768]{1,0:T(8,128)(2,1)} %get-tuple-element.142), channel_id=1, source_target_pairs={{0,1},{1,0},{2,3},{3,2},{4,5},{5,4},{6,7},{7,6},{8,9},{9,8},{10,11... | collective-permute-start | bytes 2359304 | tf_op jit(solution)/shard_map/ppermute | solution.py:676
  245.8 8.5 %collective-permute-start.37 = (bf16[104,768]{1,0:T(8,128)(2,1)S(1)}, bf16[104,768]{1,0:T(8,128)(2,1)}, u32[]{:S(2)}, u32[]{:S(2)}) collective-permute-start(bf16[104,768]{1,0:T(8,128)(2,1)S(1)} %pad_maximum_fusion.5), channel_id=1, source_target_pairs={{0,24},{4,28},{8,16},{12,20},{16,8},{20,12},{24,0},{28,4},{1,25},{... | collective-permute-start | bytes 479240 | tf_op jit(solution)/shard_map/ppermute | solution.py:682
  258.3 11.7 %collective-permute-start.39 = (f32[2,768]{1,0:T(2,128)S(1)}, f32[2,768]{1,0:T(2,128)S(1)}, u32[]{:S(2)}, u32[]{:S(2)}) collective-permute-start(f32[2,768]{1,0:T(2,128)S(1)} %add.62), channel_id=1, source_target_pairs={{0,2},{1,3},{2,0},{3,1},{4,6},{5,7},{6,4},{7,5},{8,10},{9,11},{10,... | collective-permute-start | bytes 18440 | tf_op jit(solution)/shard_map/ppermute | solution.py:679
  (57 other events, 392.9 us)
Sparse Core Ops, SparseCore 0:
  31.0 51.2 all-gather.1
  155.5 73.6 reduce-scatter.1
